TPU v7x, 32 devices: a whole 2x2x4 slice. The times are simulated.
32 devices in a mesh: ctx: 8 (over z, x), seq: 2 (over y), tp: 2 (over core).
Axes of the slice: x: 2, y: 2, z: 4, core: 2. Of those that a mesh axis runs over, the one named last changes fastest.
Arguments:
- tokens: bfloat16 [4, 1024, 1024], P('seq', 'ctx'), may hold values from -6 to 6
- positions: int32 [4, 1024], P('seq', 'ctx'), may hold values from 0 to 1023, as said below
- attn_gain: float32 [1024], replicated, may hold values from 0.5 to 1.5
- ffn_gain: float32 [1024], replicated, may hold values from 0.5 to 1.5
- q_gain: float32 [64], replicated, may hold values from 0.5 to 1.5, as said below
- k_gain: float32 [64], replicated, may hold values from 0.5 to 1.5, as said below
- w_query: bfloat16 [1024, 1024], P(None, 'tp'), may hold values from -0.1875 to 0.1875
- w_key: bfloat16 [1024, 512], P(None, 'tp'), may hold values from -0.1875 to 0.1875
- w_value: bfloat16 [1024, 512], P(None, 'tp'), may hold values from -0.1875 to 0.1875
- w_out: bfloat16 [1024, 1024], P(None, 'tp'), may hold values from -1.5 to 1.5
- w_gate: bfloat16 [1024, 4608], P(None, 'tp'), may hold values from -0.1875 to 0.1875
- w_up: bfloat16 [1024, 4608], P(None, 'tp'), may hold values from -0.1875 to 0.1875
- w_down: bfloat16 [1024, 4608], P(None, 'tp'), may hold values from -0.09375 to 0.09375
- cotangent: bfloat16 [4, 1024, 1024], P('seq', 'ctx'), may hold values from -6 to 6
Outputs:
- layer_output: float32 [4, 1024, 1024], P('seq', 'ctx')
- input_grad: float32 [4, 1024, 1024], P('seq', 'ctx')
- wq_grad: float32 [1024, 1024], P(('ctx', 'seq'), 'tp')
- wk_grad: float32 [1024, 512], P(('ctx', 'seq'), 'tp')
- wv_grad: float32 [1024, 512], P(('ctx', 'seq'), 'tp')
- wo_grad: float32 [1024, 1024], P(('ctx', 'seq'), 'tp')
- wgate_grad: float32 [1024, 4608], P(('ctx', 'seq'), 'tp')
- wup_grad: float32 [1024, 4608], P(('ctx', 'seq'), 'tp')
- wdown_grad: float32 [1024, 4608], P(('ctx', 'seq'), 'tp')
- attngain_grad: float32 [1024], P(('ctx', 'seq'))
- ffngain_grad: float32 [1024], P(('ctx', 'seq'))
- qgain_grad: float32 [64], replicated
- kgain_grad: float32 [64], replicated
Inputs may be any that keep to these rules, and one draw needn't show every extreme that they name: positions[b, i] is i minus the first index of the document that holds token i of sequence b: 0 at a document's first token and at i = 0, else one more than at i - 1; sequence 0 is one document. `q_gain`: positive entries. `k_gain`: positive entries.
All inputs are finite; a program needn't handle non-finite values.
Results may differ from a plain program's by a relative error of at most 0.011.
Values may be sent and summed in bfloat16 or wider, within the bound.
No kernel may reach another device: no remote copies, remote signals or barrier semaphores. Data moves between devices by JAX's collectives and lax.ppermute only.
A program may use at most 192 MiB of HBM per device.

v0:
```python
import functools
import math

import jax
import jax.numpy as jnp
from jax import lax
from jax.experimental import pallas as pl
from jax.experimental.pallas import tpu as pltpu
from jax.sharding import PartitionSpec as P


eps_norm = 1e-05
theta_base = 1000000.0
negative = -1e30
bf16 = jnp.bfloat16
f32 = jnp.float32
lanes = 128
pos_shift = 7
pos_base = 1 << pos_shift
pos_rows = 16


def dot_f32(lhs, rhs, lhs_dim, rhs_dim):
    return lax.dot_general(
        lhs, rhs, (((lhs_dim,), (rhs_dim,)), ((), ())), preferred_element_type=f32
    )


def rms_back(grad_in, values, stat_val):
    return stat_val * grad_in - values * stat_val**3 * jnp.mean(
        grad_in * values, axis=-1, keepdims=True
    )


def xor_swap(value, axis, flip):
    size = lax.axis_size(axis)
    return lax.ppermute(value, axis, [(index, index ^ flip) for index in range(size)])


def pick(value, index, axis=0):
    return lax.dynamic_index_in_dim(value, index, axis, keepdims=False)


def named_swap(value, axis="tp"):
    return xor_swap(value, axis, 1)


def z_exchange(blocks):
    count = blocks.shape[0]
    here = lax.axis_index("ctx") // 2
    found = [pick(blocks, here)] + [None] * (count - 1)
    for flip in range(count - 1, 0, -1):
        found[flip] = xor_swap(pick(blocks, here ^ flip), "ctx", 2 * flip)
    return found


def fill_heads(ref, place, rows, head_dim):
    tokens_count = rows.shape[0]
    for head in range(rows.shape[1] // head_dim):
        ref[place, head * tokens_count : (head + 1) * tokens_count, :] = rows[
            :, head * head_dim : (head + 1) * head_dim
        ]


def gather_blocks(order_ref, block_refs, pair_refs, query_buf, key_buf, value_buf, low_buf):
    count = len(block_refs)
    seq_count = key_buf.shape[0]
    head_dim = key_buf.shape[2]
    block_len = pair_refs[0].shape[0] // seq_count
    side = order_ref[count]
    for flip in range(count):
        level = order_ref[flip]
        block_ref = block_refs[flip]
        own_start = pl.multiple_of((level * 2 + side) * block_len, block_len)
        other_start = pl.multiple_of((level * 2 + 1 - side) * block_len, block_len)
        tail = block_ref[seq_count * block_len :, :].astype(f32)
        found = tail[:, :block_len] * pos_base + tail[:, block_len : 2 * block_len]
        token = own_start + lax.broadcasted_iota(jnp.int32, (1, block_len), 1)
        for seq in range(seq_count):
            part = slice(seq * block_len, (seq + 1) * block_len)
            fill_heads(query_buf, seq * count + level, block_ref[part, :lanes], head_dim)
            own = pl.ds(own_start, block_len)
            other = pl.ds(other_start, block_len)
            key_buf[seq, own, :] = block_ref[part, lanes : lanes + head_dim]
            value_buf[seq, own, :] = block_ref[part, lanes + head_dim :]
            key_buf[seq, other, :] = pair_refs[flip][part, :head_dim]
            value_buf[seq, other, :] = pair_refs[flip][part, head_dim:]
            low_buf[seq * count + level] = token - found[seq : seq + 1].astype(jnp.int32)


def visible(order_ref, low_row, count, level, key_count, block_len, width):
    low = jnp.concatenate([low_row] * (width // block_len), axis=1)
    shape = (key_count, low.shape[1])
    key_index = lax.broadcasted_iota(jnp.int32, shape, 0)
    lane = lax.broadcasted_iota(jnp.int32, shape, 1) % block_len
    query_index = (level * 2 + order_ref[count]) * block_len + lane
    return (key_index <= query_index) & (key_index >= low)


def unfold(turned, block_len):
    parts = [
        turned[:, start : start + block_len] for start in range(0, turned.shape[1], block_len)
    ]
    return jnp.concatenate(parts, axis=0).T


def attend_kernel(count, *refs):
    order_ref = refs[0]
    block_refs = refs[1 : 1 + count]
    pair_refs = refs[1 + count : 1 + 2 * count]
    out_ref, lse_ref, query_buf, key_buf, value_buf, low_buf = refs[1 + 2 * count :]
    gather_blocks(order_ref, block_refs, pair_refs, query_buf, key_buf, value_buf, low_buf)
    seq_count, _, head_dim = key_buf.shape
    block_len = low_buf.shape[2]
    for seq in range(seq_count):
        for level in range(count):
            place = seq * count + level
            key_count = 2 * block_len * (level + 1)
            query = query_buf[place]
            scores = dot_f32(key_buf[seq, :key_count, :], query, 1, 1) * head_dim ** (-0.5)
            allowed = visible(
                order_ref, low_buf[place], count, level, key_count, block_len, query.shape[0]
            )
            scores = jnp.where(allowed, scores, negative)
            top = jnp.max(scores, axis=0, keepdims=True)
            weights = jnp.exp(scores - top)
            row_sum = jnp.sum(weights, axis=0, keepdims=True)
            lse_ref[place : place + 1, :] = top + jnp.log(row_sum)
            turned = dot_f32(value_buf[seq, :key_count, :], weights.astype(bf16), 0, 0) / row_sum
            out_ref[level, seq * block_len : (seq + 1) * block_len, :] = unfold(
                turned, block_len
            ).astype(bf16)


def attend_back_kernel(count, *refs):
    order_ref = refs[0]
    block_refs = refs[1 : 1 + count]
    pair_refs = refs[1 + count : 1 + 2 * count]
    grad_refs = refs[1 + 2 * count : 1 + 3 * count]
    (
        out_ref,
        lse_ref,
        query_grad_ref,
        own_ref,
        other_ref,
        query_buf,
        key_buf,
        value_buf,
        low_buf,
        grad_buf,
        key_acc,
        value_acc,
    ) = refs[1 + 3 * count :]
    gather_blocks(order_ref, block_refs, pair_refs, query_buf, key_buf, value_buf, low_buf)
    seq_count, _, head_dim = key_buf.shape
    block_len = low_buf.shape[2]
    group = lanes // head_dim
    for flip in range(count):
        for seq in range(seq_count):
            rows = grad_refs[flip][seq * block_len : (seq + 1) * block_len, :]
            fill_heads(grad_buf, seq * count + order_ref[flip], rows, head_dim)
    key_acc[...] = jnp.zeros_like(key_acc)
    value_acc[...] = jnp.zeros_like(value_acc)
    scale = head_dim ** (-0.5)
    ones_row = jnp.ones((8, head_dim), f32)
    for seq in range(seq_count):
        for level in range(count):
            place = seq * count + level
            key_count = 2 * block_len * (level + 1)
            keys = key_buf[seq, :key_count, :]
            query = query_buf[place]
            grad = grad_buf[place]
            rows = out_ref[level, seq * block_len : (seq + 1) * block_len, :]
            out = jnp.concatenate(
                [rows[:, head * head_dim : (head + 1) * head_dim] for head in range(group)], axis=0
            )
            delta = lax.dot_general(
                ones_row,
                grad.astype(f32) * out.astype(f32),
                (((1,), (1,)), ((), ())),
                precision=lax.Precision.HIGHEST,
                preferred_element_type=f32,
            )[:1, :]
            scores = dot_f32(keys, query, 1, 1) * scale
            allowed = visible(
                order_ref, low_buf[place], count, level, key_count, block_len, query.shape[0]
            )
            probs = jnp.where(allowed, jnp.exp(scores - lse_ref[place : place + 1, :]), 0.0)
            grad_probs = dot_f32(value_buf[seq, :key_count, :], grad, 1, 1)
            grad_scores = (probs * (grad_probs - delta)).astype(bf16)
            value_acc[seq, :key_count, :] += dot_f32(probs.astype(bf16), grad, 1, 0)
            key_acc[seq, :key_count, :] += dot_f32(grad_scores, query, 1, 0)
            turned = dot_f32(keys, grad_scores, 0, 0) * scale
            query_grad_ref[level, seq * block_len : (seq + 1) * block_len, :] = unfold(
                turned, block_len
            ).astype(bf16)
    side = order_ref[count]
    for seq in range(seq_count):
        part = slice(seq * block_len, (seq + 1) * block_len)
        for level in range(count):
            for ref, place in ((own_ref, side), (other_ref, 1 - side)):
                start = pl.multiple_of((2 * level + place) * block_len, block_len)
                rows = pl.ds(start, block_len)
                both = [key_acc[seq, rows, :] * scale, value_acc[seq, rows, :]]
                ref[level, part, :] = jnp.concatenate(both, axis=1).astype(ref.dtype)


def merge_kernel(query_ref, own_ref, other_ref, out_ref):
    out_ref[:, :, :lanes] = query_ref[...]
    out_ref[:, :, lanes:] = (own_ref[...] + other_ref[...].astype(f32)).astype(bf16)


def smem_spec():
    return pl.BlockSpec(memory_space=pltpu.SMEM)


def vmem_spec():
    return pl.BlockSpec(memory_space=pltpu.VMEM)


def shape_of(shape, dtype):
    return jax.ShapeDtypeStruct(shape, dtype)


def whole_call(kernel, outs, args, scalars=(), scratch=(), flops=0):
    moved = sum(arg.size * arg.dtype.itemsize for arg in args)
    moved += sum(out.size * jnp.dtype(out.dtype).itemsize for out in outs)
    return pl.pallas_call(
        kernel,
        out_shape=tuple(outs),
        in_specs=[smem_spec()] * len(scalars) + [vmem_spec()] * len(args),
        out_specs=tuple(vmem_spec() for _ in outs),
        scratch_shapes=list(scratch),
        cost_estimate=pl.CostEstimate(flops=flops, bytes_accessed=moved, transcendentals=0),
    )(*scalars, *args)


def head_scratch(seq_count, count, block_len, head_dim):
    total = 2 * count * block_len
    heads_rows = lanes // head_dim * block_len
    return [
        pltpu.VMEM((seq_count * count, heads_rows, head_dim), bf16),
        pltpu.VMEM((seq_count, total, head_dim), bf16),
        pltpu.VMEM((seq_count, total, head_dim), bf16),
        pltpu.VMEM((seq_count * count, 1, block_len), jnp.int32),
    ]


def head_forward(order, blocks, pairs, seq_count, head_dim):
    count = len(blocks)
    row_count = pairs[0].shape[0]
    block_len = row_count // seq_count
    heads_rows = lanes // head_dim * block_len
    return whole_call(
        functools.partial(attend_kernel, count),
        [
            shape_of((count, row_count, lanes), bf16),
            shape_of((seq_count * count, heads_rows), f32),
        ],
        [*blocks, *pairs],
        scalars=(order,),
        scratch=head_scratch(seq_count, count, block_len, head_dim),
        flops=8 * row_count * row_count * count * count * lanes,
    )


def head_backward(order, blocks, pairs, grads, out, log_sum, seq_count, head_dim):
    count = len(blocks)
    row_count = pairs[0].shape[0]
    block_len = row_count // seq_count
    heads_rows = lanes // head_dim * block_len
    total = 2 * count * block_len
    return whole_call(
        functools.partial(attend_back_kernel, count),
        [
            shape_of((count, row_count, lanes), bf16),
            shape_of((count, row_count, lanes), f32),
            shape_of((count, row_count, lanes), bf16),
        ],
        [*blocks, *pairs, *grads, out, log_sum],
        scalars=(order,),
        scratch=head_scratch(seq_count, count, block_len, head_dim)
        + [
            pltpu.VMEM((seq_count * count, heads_rows, head_dim), bf16),
            pltpu.VMEM((seq_count, total, head_dim), f32),
            pltpu.VMEM((seq_count, total, head_dim), f32),
        ],
        flops=20 * row_count * row_count * count * count * lanes,
    )


def gathered_scores(query_grouped, key_piece, query_pos, lowest_pos, key_pos):
    head_dim = query_grouped.shape[-1]
    keys_split = key_piece.reshape(
        key_piece.shape[0], key_piece.shape[1], query_grouped.shape[2], head_dim
    )
    scores = jnp.einsum(
        "sqhgd,skhd->shgqk", query_grouped, keys_split, preferred_element_type=f32
    ) * head_dim ** (-0.5)
    allowed = (key_pos[None, None, :] <= query_pos[None, :, None]) & (
        key_pos[None, None, :] >= lowest_pos[:, :, None]
    )
    allowed = allowed[:, None, None, :, :]
    return (jnp.where(allowed, scores, negative), allowed, keys_split)


def gathered_forward(query_grouped, key_rows, value_rows, query_index, lowest_key):
    key_all = lax.all_gather(key_rows, "ctx", axis=1, tiled=True)
    value_all = lax.all_gather(value_rows, "ctx", axis=1, tiled=True)
    key_pos = jnp.arange(key_all.shape[1], dtype=jnp.int32)
    scores, allowed, keys_split = gathered_scores(
        query_grouped, key_all, query_index, lowest_key, key_pos
    )
    top = jnp.max(scores, axis=-1)
    weights = jnp.where(allowed, jnp.exp(scores - top[..., None]), 0.0)
    row_sum = jnp.sum(weights, axis=-1)
    summed = jnp.einsum(
        "shgqk,skhd->shgqd",
        weights.astype(bf16),
        value_all.reshape(keys_split.shape),
        preferred_element_type=f32,
    )
    attended = (summed / row_sum[..., None]).astype(bf16)
    return (jnp.transpose(attended, (0, 3, 1, 2, 4)), top + jnp.log(row_sum), key_all, value_all)


def gathered_backward(
    query_grouped, grad_grouped, attended, log_sum, key_all, value_all, query_index, lowest_key
):
    scale = query_grouped.shape[-1] ** (-0.5)
    key_pos = jnp.arange(key_all.shape[1], dtype=jnp.int32)
    delta_rows = jnp.sum(grad_grouped.astype(f32) * attended.astype(f32), axis=-1)
    delta_stat = jnp.transpose(delta_rows, (0, 2, 3, 1))
    scores, allowed, keys_split = gathered_scores(
        query_grouped, key_all, query_index, lowest_key, key_pos
    )
    probs = jnp.where(allowed, jnp.exp(scores - log_sum[..., None]), 0.0)
    grad_probs = jnp.einsum(
        "sqhgd,skhd->shgqk",
        grad_grouped,
        value_all.reshape(keys_split.shape),
        preferred_element_type=f32,
    )
    grad_scores = (probs * (grad_probs - delta_stat[..., None])).astype(bf16)
    query_grad = (
        jnp.einsum("shgqk,skhd->sqhgd", grad_scores, keys_split, preferred_element_type=f32) * scale
    )
    key_grad = (
        jnp.einsum("shgqk,sqhgd->skhd", grad_scores, query_grouped, preferred_element_type=f32)
        * scale
    )
    value_grad = jnp.einsum(
        "shgqk,sqhgd->skhd", probs.astype(bf16), grad_grouped, preferred_element_type=f32
    )
    key_own, value_own = (
        lax.psum_scatter(part.reshape(key_all.shape), "ctx", scatter_dimension=1, tiled=True)
        for part in (key_grad, value_grad)
    )
    return (query_grad, key_own, value_own)


def split_dot(value, table):
    high = value.astype(bf16)
    low = (value - high.astype(f32)).astype(bf16)
    return dot_f32(high, table, 1, 0) + dot_f32(low, table, 1, 0)


def head_table(head_dim):
    row = lax.broadcasted_iota(jnp.int32, (lanes, lanes), 0) // head_dim
    col = lax.broadcasted_iota(jnp.int32, (lanes, lanes), 1) // head_dim
    return jnp.where(row == col, 1.0 / head_dim, 0.0).astype(bf16)


def swap_halves(value, head_dim):
    lane = lax.broadcasted_iota(jnp.int32, value.shape, 1)
    ahead = pltpu.roll(value, lanes - head_dim // 2, 1)
    behind = pltpu.roll(value, head_dim // 2, 1)
    return jnp.where(lane % head_dim < head_dim // 2, ahead, behind)


def front_kernel(
    head_dim,
    tokens_ref,
    gain_ref,
    query_w_ref,
    key_w_ref,
    value_w_ref,
    q_gain_ref,
    k_gain_ref,
    pos_ref,
    blocks_ref,
    normed_ref,
    query_ref,
    key_ref,
    cos_ref,
    sin_ref,
):
    seq_count, block_len = pos_ref.shape
    half_dim = head_dim // 2
    places = pos_ref[...]
    spare = jnp.zeros((8 - seq_count, block_len), f32)
    columns = jnp.concatenate([places.astype(f32), spare], axis=0).T
    lane_row = lax.broadcasted_iota(jnp.int32, (1, lanes), 1)
    exponent = (lane_row % half_dim).astype(f32) * (-2.0 / head_dim)
    frequency = jnp.exp(exponent * math.log(theta_base))
    sign = jnp.where(lane_row % head_dim < half_dim, -1.0, 1.0)
    for seq in range(seq_count):
        angles = columns[:, seq : seq + 1] * frequency
        cos_ref[seq * block_len : (seq + 1) * block_len, :] = jnp.cos(angles)
        sin_ref[seq * block_len : (seq + 1) * block_len, :] = jnp.sin(angles) * sign
    packed_pos = jnp.concatenate([places >> pos_shift, places & (pos_base - 1)], axis=1).astype(f32)
    fill = jnp.zeros((pos_rows - seq_count, packed_pos.shape[1]), f32)
    pos_tail = jnp.concatenate([packed_pos, fill], axis=0).astype(bf16)
    q_gain_row = jnp.concatenate([q_gain_ref[...]] * (lanes // head_dim), axis=1)
    k_gain_row = jnp.concatenate([k_gain_ref[...]] * (lanes // head_dim), axis=1)
    rows = tokens_ref[...].astype(f32)
    stat = lax.rsqrt(jnp.mean(rows * rows, axis=1, keepdims=True) + eps_norm)
    normed = (rows * stat * gain_ref[...]).astype(bf16)
    normed_ref[...] = normed
    query = dot_f32(normed, query_w_ref[...], 1, 0)
    key = dot_f32(normed, key_w_ref[...], 1, 0)
    value = dot_f32(normed, value_w_ref[...], 1, 0).astype(bf16).astype(f32)
    query_ref[...] = query
    key_ref[...] = key
    table = head_table(head_dim)
    cosine = cos_ref[...]
    sine = sin_ref[...]
    kv_heads = key.shape[1] // head_dim
    lane = lax.broadcasted_iota(jnp.int32, (rows.shape[0], lanes), 1)

    def turned(tile, gain):
        stat_val = lax.rsqrt(split_dot(tile * tile, table) + eps_norm)
        scaled = tile * stat_val * gain
        return scaled * cosine + swap_halves(scaled, head_dim) * sine

    for head in range(kv_heads):
        query_tile = turned(query[:, head * lanes : (head + 1) * lanes], q_gain_row).astype(bf16)
        pair = slice(head // 2 * lanes, (head // 2 + 1) * lanes)
        key_tile = turned(key[:, pair], k_gain_row)
        value_tile = value[:, pair]
        if head % 2 == 0:
            value_tile = pltpu.roll(value_tile, head_dim, 1)
        else:
            key_tile = pltpu.roll(key_tile, head_dim, 1)
        both = jnp.where(lane < head_dim, key_tile, value_tile).astype(bf16)
        row_count = rows.shape[0]
        blocks_ref[head, :row_count, :lanes] = query_tile
        blocks_ref[head, :row_count, lanes:] = both
        blocks_ref[head, row_count:, :] = pos_tail


def project_kernel(order_ref, *refs):
    count = len(refs) - 3
    block_refs = refs[:count]
    weight_ref, heads_ref, part_ref = refs[count:]
    for flip in range(count):
        heads_ref[order_ref[flip]] = block_refs[flip][...]
    total = None
    for head in range(count):
        found = dot_f32(heads_ref[head], weight_ref[:, head * lanes : (head + 1) * lanes], 1, 1)
        total = found if total is None else total + found
    part_ref[...] = total.astype(bf16)


def ffn_kernel(
    steps,
    tokens_ref,
    own_ref,
    other_ref,
    gain_ref,
    cot_ref,
    gate_ref,
    up_ref,
    down_ref,
    mixed_ref,
    normed_ref,
    hidden_ref,
    both_ref,
    ffn_ref,
    back_ref,
    ffn_acc,
    back_acc,
):
    step = pl.program_id(0)

    @pl.when(step == 0)
    def _():
        mixed = tokens_ref[...].astype(f32) + (own_ref[...].astype(f32) + other_ref[...].astype(f32))
        mixed_ref[...] = mixed
        stat = lax.rsqrt(jnp.mean(mixed * mixed, axis=1, keepdims=True) + eps_norm)
        normed_ref[...] = (mixed * stat * gain_ref[...]).astype(bf16)
        ffn_acc[...] = jnp.zeros_like(ffn_acc)
        back_acc[...] = jnp.zeros_like(back_acc)

    normed = normed_ref[...]
    gate = dot_f32(normed, gate_ref[...], 1, 0)
    up = dot_f32(normed, up_ref[...], 1, 0)
    grad = dot_f32(cot_ref[...], down_ref[...], 1, 0)
    sig = jax.nn.sigmoid(gate)
    silu = gate * sig
    hidden = (silu * up).astype(bf16)
    hidden_ref[...] = hidden
    grad_gate = (grad * up * (sig * (1.0 + gate * (1.0 - sig)))).astype(bf16)
    grad_up = (grad * silu).astype(bf16)
    both_ref[0, 0] = grad_gate
    both_ref[0, 1] = grad_up
    ffn_acc[...] += dot_f32(hidden, down_ref[...], 1, 1)
    back_acc[...] += dot_f32(grad_gate, gate_ref[...], 1, 1) + dot_f32(grad_up, up_ref[...], 1, 1)

    @pl.when(step == steps - 1)
    def _():
        ffn_ref[...] = ffn_acc[...].astype(bf16)
        back_ref[...] = back_acc[...].astype(bf16)


def ffn_call(tokens_in, own, other, gain, cot, w_gate, w_up, w_down):
    row_count, model_width = tokens_in.shape
    cols = w_gate.shape[1]
    half = cols // 2
    tile = half
    while tile > 384 and (tile // lanes) % 3 == 0:
        tile //= 3
    steps = cols // tile
    per_half = half // tile
    fixed = lambda *shape: pl.BlockSpec(shape, lambda step: (0,) * len(shape))
    moving = pl.BlockSpec((model_width, tile), lambda step: (0, step))
    rows_spec = fixed(row_count, model_width)
    return pl.pallas_call(
        functools.partial(ffn_kernel, steps),
        grid=(steps,),
        out_shape=(
            shape_of((row_count, model_width), f32),
            shape_of((row_count, model_width), bf16),
            shape_of((row_count, cols), bf16),
            shape_of((2, 2, row_count, half), bf16),
            shape_of((row_count, model_width), bf16),
            shape_of((row_count, model_width), bf16),
        ),
        in_specs=[rows_spec, rows_spec, rows_spec, fixed(1, model_width), rows_spec]
        + [moving] * 3,
        out_specs=(
            rows_spec,
            rows_spec,
            pl.BlockSpec((row_count, tile), lambda step: (0, step)),
            pl.BlockSpec(
                (1, 2, row_count, tile), lambda step: (step // per_half, 0, 0, step % per_half)
            ),
            rows_spec,
            rows_spec,
        ),
        scratch_shapes=[pltpu.VMEM((row_count, model_width), f32)] * 2,
        cost_estimate=pl.CostEstimate(
            flops=16 * row_count * model_width * cols,
            bytes_accessed=6 * model_width * cols,
            transcendentals=row_count * cols,
        ),
        name="ffn",
    )(tokens_in, own, other, gain, cot, w_gate, w_up, w_down)


def middle_kernel(
    mixed_ref,
    ffn_own_ref,
    ffn_other_ref,
    back_own_ref,
    back_other_ref,
    gain_ref,
    cot_ref,
    weight_ref,
    layer_ref,
    grad_ref,
    rounded_ref,
    blocks_ref,
    row_ref,
):
    mixed = mixed_ref[...]
    layer_ref[...] = mixed + (ffn_own_ref[...].astype(f32) + ffn_other_ref[...].astype(f32))
    found = back_own_ref[...].astype(f32) + back_other_ref[...].astype(f32)
    stat = lax.rsqrt(jnp.mean(mixed * mixed, axis=1, keepdims=True) + eps_norm)
    row_ref[...] = jnp.broadcast_to(
        jnp.sum(found * mixed * stat, axis=0, keepdims=True), row_ref.shape
    )
    grad = cot_ref[...].astype(f32) + rms_back(found * gain_ref[...], mixed, stat)
    grad_ref[...] = grad
    rounded = grad.astype(bf16)
    rounded_ref[...] = rounded
    attended = dot_f32(rounded, weight_ref[...], 1, 0).astype(bf16)
    for head in range(blocks_ref.shape[0]):
        blocks_ref[head] = attended[:, head * lanes : (head + 1) * lanes]


def turn_back_kernel(head_dim, order_ref, *refs):
    count = len(refs) - 14
    block_refs = refs[:count]
    (
        query_ref,
        key_ref,
        q_gain_ref,
        k_gain_ref,
        cos_ref,
        sin_ref,
        query_w_ref,
        key_w_ref,
        value_w_ref,
        raw_ref,
        part_ref,
        gain_row_ref,
        query_buf,
        pair_buf,
    ) = refs[count:]
    kv_heads = count
    for flip in range(count):
        query_buf[order_ref[flip]] = block_refs[flip][:, :lanes]
        pair_buf[order_ref[flip]] = block_refs[flip][:, lanes:]
    table = head_table(head_dim)
    cosine = cos_ref[...]
    sine = sin_ref[...]
    q_gain_row = jnp.concatenate([q_gain_ref[...]] * (lanes // head_dim), axis=1)
    k_gain_row = jnp.concatenate([k_gain_ref[...]] * (lanes // head_dim), axis=1)
    lane = lax.broadcasted_iota(jnp.int32, cosine.shape, 1)

    def back(grad_rot, raw, gain):
        grad_norm = grad_rot * cosine - swap_halves(grad_rot, head_dim) * sine
        stat = lax.rsqrt(split_dot(raw * raw, table) + eps_norm)
        gain_row = jnp.sum(grad_norm * raw * stat, axis=0, keepdims=True)
        grad_in = grad_norm * gain
        grad_raw = stat * grad_in - raw * stat**3 * split_dot(grad_in * raw, table)
        return (grad_raw.astype(bf16), gain_row)

    total = None
    gain_rows = [None, None]
    place = 0
    per_slot = raw_ref.shape[2] // lanes

    def emit(tile, weight, kind, gain_row):
        nonlocal total, place
        slot = place % per_slot
        raw_ref[place // per_slot, :, slot * lanes : (slot + 1) * lanes] = tile
        place += 1
        found = dot_f32(tile, weight, 1, 1)
        total = found if total is None else total + found
        if gain_row is not None:
            gain_rows[kind] = gain_row if gain_rows[kind] is None else gain_rows[kind] + gain_row

    for head in range(kv_heads):
        cols = slice(head * lanes, (head + 1) * lanes)
        tile, gain_row = back(query_buf[head].astype(f32), query_ref[:, cols], q_gain_row)
        emit(tile, query_w_ref[:, cols], 0, gain_row)
    for pair in range(kv_heads // 2):
        cols = slice(pair * lanes, (pair + 1) * lanes)
        first = pair_buf[2 * pair].astype(f32)
        second = pair_buf[2 * pair + 1].astype(f32)
        merged = jnp.where(lane < head_dim, first, pltpu.roll(second, head_dim, 1))
        tile, gain_row = back(merged, key_ref[:, cols], k_gain_row)
        emit(tile, key_w_ref[:, cols], 1, gain_row)
    for pair in range(kv_heads // 2):
        cols = slice(pair * lanes, (pair + 1) * lanes)
        first = pair_buf[2 * pair].astype(f32)
        second = pair_buf[2 * pair + 1].astype(f32)
        merged = jnp.where(lane < head_dim, pltpu.roll(first, head_dim, 1), second).astype(bf16)
        emit(merged, value_w_ref[:, cols], 1, None)
    part_ref[...] = total.astype(bf16)
    gain_row_ref[...] = jnp.concatenate(
        gain_rows + [jnp.zeros((6, lanes), f32)], axis=0
    )


def last_kernel(tokens_ref, grad_ref, own_ref, other_ref, gain_ref, out_ref, row_ref):
    rows = tokens_ref[...].astype(f32)
    stat = lax.rsqrt(jnp.mean(rows * rows, axis=1, keepdims=True) + eps_norm)
    found = own_ref[...].astype(f32) + other_ref[...].astype(f32)
    row_ref[...] = jnp.broadcast_to(
        jnp.sum(found * rows * stat, axis=0, keepdims=True), row_ref.shape
    )
    out_ref[...] = grad_ref[...] + rms_back(found * gain_ref[...], rows, stat)


everywhere = ("ctx", "seq")
plane = 4


def plane_gather(mine):
    near = [xor_swap(mine, everywhere, flip) for flip in range(1, plane)]
    far = [xor_swap(found, "tp", 1) for found in near]
    return (near, far)


def half_of(rows, core):
    half = rows.shape[0] // 2
    return lax.dynamic_slice_in_dim(rows, core * half, half, 0)


def window(cols):
    half = cols // 2
    width = min(half, -(-half // (2 * lanes)) * lanes)
    return (half, width)


def plane_exchange(take, place):
    parts = [take(place)]
    for flip in range(1, plane):
        parts.append(xor_swap(take(place ^ flip), everywhere, flip))
    return parts


def rows_kernel(scalars_ref, own_ref, *refs):
    near_refs = refs[: plane - 1]
    far_refs = refs[plane - 1 : 2 * plane - 2]
    col_refs = refs[2 * plane - 2 : 3 * plane - 2]
    out_ref, row_buf = refs[3 * plane - 2 :]
    step = pl.program_id(0)
    row_count = own_ref.shape[0]
    half = row_count // 2
    height = out_ref.shape[1]
    core = scalars_ref[0]
    start = pl.multiple_of((scalars_ref[1] + step * scalars_ref[2]) * height, height)
    cols = pl.ds(start, height)
    row_buf[:row_count, :] = own_ref[:, cols]
    for n in range(plane - 1):
        base = (n + 1) * row_count
        near_rows = pl.ds(pl.multiple_of(base + core * half, half), half)
        far_rows = pl.ds(pl.multiple_of(base + (1 - core) * half, half), half)
        row_buf[near_rows, :] = near_refs[n][:, cols]
        row_buf[far_rows, :] = far_refs[n][:, cols]
    total = None
    for n in range(plane):
        found = dot_f32(row_buf[n * row_count : (n + 1) * row_count, :], col_refs[n][...], 0, 0)
        total = found if total is None else total + found
    out_ref[0] = total.astype(out_ref.dtype)


def rows_call(row_pieces, col_parts, scalars, steps, height, dtype):
    own, near, far, slot = row_pieces
    row_count, model_width = own.shape
    half = row_count // 2
    width = col_parts[0].shape[1]
    fixed = lambda *shape: pl.BlockSpec(shape, lambda step: (0,) * len(shape))
    return pl.pallas_call(
        rows_kernel,
        grid=(steps,),
        out_shape=shape_of((steps, height, width), dtype),
        in_specs=[smem_spec(), fixed(row_count, model_width)]
        + [pl.BlockSpec((half, model_width), lambda step: (0, slot))] * (2 * plane - 2)
        + [fixed(row_count, width)] * plane,
        out_specs=pl.BlockSpec((1, height, width), lambda step: (step, 0, 0)),
        scratch_shapes=[pltpu.VMEM((plane * row_count, height), bf16)],
        cost_estimate=pl.CostEstimate(
            flops=2 * plane * row_count * steps * height * width,
            bytes_accessed=2 * plane * row_count * (model_width + width)
            + 4 * steps * height * width,
            transcendentals=0,
        ),
        name="rows",
    )(scalars, own, *near, *far, *col_parts)


class Halving:
    def __init__(self, index, core, total, model_width):
        self.blocks = total // plane
        self.bits = self.blocks.bit_length() - 1
        self.block_index = index // plane
        self.core = core
        self.fine = model_width // self.blocks % lanes == 0
        self.order = list(range(self.bits))
        if self.fine:
            self.steps, self.height, self.scale = self.blocks // 2, model_width // self.blocks, 2
        else:
            self.order.reverse()
            self.steps, self.height, self.scale = 1, model_width // 2, 1
        self.first = (self.block_index >> self.order[0]) & 1

    def rows(self, row_pieces, col_parts, mine):
        bit = self.first if mine else 1 - self.first
        scalars = jnp.stack([self.core, bit, jnp.int32(self.scale)]).astype(jnp.int32)
        dtype = f32 if mine else bf16
        return rows_call(row_pieces, col_parts, scalars, self.steps, self.height, dtype)

    def split(self, value):
        shaped = value.reshape(self.steps, 2, self.height, -1)
        return (pick(shaped, 1 - self.first, 1).astype(bf16), pick(shaped, self.first, 1))

    def start(self, sent):
        return xor_swap(sent, everywhere, plane << self.order[0])

    def finish(self, kept, found):
        kept = kept + found.astype(f32)
        width = kept.shape[2]
        for turn, bit in enumerate(self.order[1:]):
            own_bit = (self.block_index >> bit) & 1
            if self.fine:
                shaped = kept.reshape(self.steps >> (turn + 1), 2, self.height, width)
            else:
                shaped = kept.reshape(1, 2, -1, width)
            sent = pick(shaped, 1 - own_bit, 1).astype(bf16)
            kept = pick(shaped, own_bit, 1)
            found = xor_swap(sent, everywhere, plane << bit)
            kept = kept + found.astype(f32)
        return kept.reshape(-1, width)


def return_rows(summed, place):
    width = summed.shape[1]
    shaped = summed.reshape(plane, -1, width)
    found = [pick(shaped, place)]
    for flip in range(1, plane):
        sent = pick(shaped, place ^ flip).astype(bf16)
        found.append(xor_swap(sent, everywhere, flip))
    return found


def assemble_kernel(moves, order_ref, *refs):
    part_refs = refs[:plane]
    out_refs = refs[plane:]
    for flip in range(plane):
        for member in range(plane):

            @pl.when(order_ref[flip] == member)
            def _():
                for out, out_start, start, width in moves[member]:
                    out_refs[out][:, out_start : out_start + width] = part_refs[flip][
                        :, start : start + width
                    ].astype(f32)


def assemble(parts, order, moves, widths):
    height = parts[0].shape[0]
    return whole_call(
        functools.partial(assemble_kernel, moves),
        [shape_of((height, width), f32) for width in widths],
        parts,
        scalars=(order,),
    )


def shards(
    tokens,
    positions,
    attn_gain,
    ffn_gain,
    q_gain,
    k_gain,
    w_query,
    w_key,
    w_value,
    w_out,
    w_gate,
    w_up,
    w_down,
    cotangent,
):
    seq_count, block_len, model_width = tokens.shape
    row_count = seq_count * block_len
    head_dim = q_gain.shape[0]
    q_heads = w_query.shape[1] // head_dim
    kv_heads = w_key.shape[1] // head_dim
    key_width = kv_heads * head_dim
    query_width = q_heads * head_dim
    group_size = q_heads // kv_heads
    hidden_width = w_gate.shape[1]
    ctx_size = lax.axis_size("ctx")
    total = ctx_size * lax.axis_size("seq")
    here_index = lax.axis_index("ctx")
    index = lax.axis_index(everywhere)
    core = lax.axis_index("tp")
    place = index % plane
    by_head = ctx_size == 2 * kv_heads
    natural = jnp.arange(kv_heads, dtype=jnp.int32)
    level_order = (here_index // 2) ^ natural if by_head else natural
    order = jnp.concatenate([level_order, (here_index % 2)[None]]).astype(jnp.int32)
    plane_order = place ^ jnp.arange(plane, dtype=jnp.int32)
    rows_bf = shape_of((row_count, model_width), bf16)
    rows_f32 = shape_of((row_count, model_width), f32)
    halving = Halving(index, core, total, model_width)

    cot_rows = cotangent.reshape(row_count, model_width)
    token_rows = tokens.reshape(row_count, model_width)

    pack_width = 2 * lanes
    q_gain_row = q_gain[None, :]
    k_gain_row = k_gain[None, :]
    attn_gain_row = attn_gain[None, :]
    ffn_gain_row = ffn_gain[None, :]

    packed, normed_one, query_raw, key_raw, cosine, sine = whole_call(
        functools.partial(front_kernel, head_dim),
        [
            shape_of((kv_heads, row_count + pos_rows, pack_width), bf16),
            rows_bf,
            shape_of((row_count, query_width), f32),
            shape_of((row_count, key_width), f32),
            shape_of((row_count, lanes), f32),
            shape_of((row_count, lanes), f32),
        ],
        [
            token_rows,
            attn_gain_row,
            w_query,
            w_key,
            w_value,
            q_gain_row,
            k_gain_row,
            positions,
        ],
        flops=2 * row_count * model_width * (query_width + 2 * key_width),
    )

    if by_head:
        blocks = z_exchange(packed)
        pairs = [xor_swap(block[:row_count, lanes:], "ctx", 1) for block in blocks]
        out_heads, log_sum = head_forward(order, blocks, pairs, seq_count, head_dim)
        out_blocks = z_exchange(out_heads)
    else:
        flat = packed[:, :row_count].reshape(kv_heads, seq_count, block_len, pack_width)
        flat = jnp.transpose(flat, (1, 2, 0, 3))
        query_grouped = flat[..., :lanes].reshape(
            seq_count, block_len, kv_heads, group_size, head_dim
        )
        query_index = here_index * block_len + jnp.arange(block_len, dtype=jnp.int32)
        lowest_key = query_index[None, :] - positions
        attended_grouped, log_sum, key_all, value_all = gathered_forward(
            query_grouped,
            flat[..., lanes : lanes + head_dim].reshape(seq_count, block_len, key_width),
            flat[..., lanes + head_dim :].reshape(seq_count, block_len, key_width),
            query_index,
            lowest_key,
        )
        out_blocks = list(
            jnp.transpose(attended_grouped, (2, 0, 1, 3, 4)).reshape(kv_heads, row_count, lanes)
        )

    early_half = jnp.concatenate([half_of(cot_rows, core), half_of(normed_one, core)], axis=1)
    early_near, early_far = plane_gather(early_half)
    cot_pieces = (cot_rows, early_near, early_far, 0)
    one_pieces = (normed_one, early_near, early_far, 1)

    heads, attn_part = whole_call(
        project_kernel,
        [shape_of((kv_heads, row_count, lanes), bf16), rows_bf],
        [*out_blocks, w_out],
        scalars=(order,),
        flops=2 * row_count * model_width * query_width,
    )
    mixed, normed_two, hidden, both_pre, ffn_part, back_part = ffn_call(
        token_rows,
        attn_part,
        named_swap(attn_part),
        ffn_gain_row,
        cot_rows,
        w_gate,
        w_up,
        w_down,
    )
    ffn_other = named_swap(ffn_part)
    back_other = named_swap(back_part)
    half, width = window(hidden_width)
    both_flat = both_pre.reshape(plane, row_count, half)
    both_plane = plane_exchange(lambda member: pick(both_flat, member), place)
    two_near, two_far = plane_gather(half_of(normed_two, core))
    two_pieces = (normed_two, two_near, two_far, 0)

    def take_hidden(member):
        start = (member % 2) * half + (member // 2) * (half - width)
        return lax.dynamic_slice_in_dim(hidden, start, width, 1)

    hidden_plane = plane_exchange(take_hidden, place)

    layer_output, grad_mixed, grad_mixed_bf, grad_blocks, ffn_row = whole_call(
        middle_kernel,
        [
            rows_f32,
            rows_f32,
            rows_bf,
            shape_of((kv_heads, row_count, lanes), bf16),
            shape_of((8, model_width), f32),
        ],
        [
            mixed,
            ffn_part,
            ffn_other,
            back_part,
            back_other,
            ffn_gain_row,
            cot_rows,
            w_out,
        ],
        flops=2 * row_count * model_width * query_width,
    )

    if by_head:
        grads = z_exchange(grad_blocks)
        query_grads, own_grads, other_grads = head_backward(
            order, blocks, pairs, grads, out_heads, log_sum, seq_count, head_dim
        )
        (packed_grads,) = whole_call(
            merge_kernel,
            [shape_of((kv_heads, row_count, pack_width), bf16)],
            [query_grads, own_grads, named_swap(other_grads, "ctx")],
        )
        returned = z_exchange(packed_grads)
    else:
        grad_grouped = jnp.transpose(
            grad_blocks.reshape(kv_heads, seq_count, block_len, group_size, head_dim),
            (1, 2, 0, 3, 4),
        )
        query_grad, key_grad_own, value_grad_own = gathered_backward(
            query_grouped,
            grad_grouped,
            attended_grouped,
            log_sum,
            key_all,
            value_all,
            query_index,
            lowest_key,
        )
        shaped = lambda grad: grad.reshape(seq_count, block_len, kv_heads, -1)
        returned = jnp.concatenate(
            [shaped(query_grad), shaped(key_grad_own), shaped(value_grad_own)], axis=-1
        ).astype(bf16)
        returned = list(
            jnp.transpose(returned, (2, 0, 1, 3)).reshape(kv_heads, row_count, pack_width)
        )

    both_found = halving.start(halving.rows(two_pieces, both_plane, False))
    both_kept = halving.rows(two_pieces, both_plane, True)
    down_found = halving.start(halving.rows(cot_pieces, hidden_plane, False))
    down_kept = halving.rows(cot_pieces, hidden_plane, True)

    mixed_half = half_of(grad_mixed_bf, core)
    mixed_near, mixed_far = plane_gather(mixed_half)
    mixed_pieces = (grad_mixed_bf, mixed_near, mixed_far, 0)
    attended_plane = plane_exchange(lambda member: pick(heads, member), place)

    raw_width = (query_width + 2 * key_width) // plane
    grad_raw, one_part, head_rows = whole_call(
        functools.partial(turn_back_kernel, head_dim),
        [
            shape_of((plane, row_count, raw_width), bf16),
            rows_bf,
            shape_of((8, lanes), f32),
        ],
        [
            *returned,
            query_raw,
            key_raw,
            q_gain_row,
            k_gain_row,
            cosine,
            sine,
            w_query,
            w_key,
            w_value,
        ],
        scalars=(order,),
        scratch=[
            pltpu.VMEM((kv_heads, row_count, lanes), bf16),
            pltpu.VMEM((kv_heads, row_count, lanes), bf16),
        ],
        flops=2 * row_count * model_width * (query_width + 2 * key_width),
    )
    raw_plane = plane_exchange(lambda member: pick(grad_raw, member), place)
    input_grad, attn_row = whole_call(
        last_kernel,
        [rows_f32, shape_of((8, model_width), f32)],
        [token_rows, grad_mixed, one_part, named_swap(one_part), attn_gain_row],
    )

    tiles = model_width // head_dim
    folded = head_rows[:2].reshape(2, lanes // head_dim, head_dim).sum(axis=1)
    gain_rows = jnp.concatenate([ffn_row[:1], attn_row[:1], jnp.tile(folded, (1, tiles))], axis=0)
    gain_cols = jnp.pad(gain_rows.T, ((0, 0), (0, lanes - 4)))
    gain_sent, gain_kept = halving.split(gain_cols)
    out_width = lanes
    late_sent = jnp.concatenate(
        [
            halving.rows(mixed_pieces, attended_plane, False),
            halving.rows(one_pieces, raw_plane, False),
            gain_sent,
        ],
        axis=2,
    )
    late_found = halving.start(late_sent)
    late_kept = jnp.concatenate(
        [
            halving.rows(mixed_pieces, attended_plane, True),
            halving.rows(one_pieces, raw_plane, True),
            gain_kept,
        ],
        axis=2,
    )

    both_sum = halving.finish(both_kept, both_found)
    down_sum = halving.finish(down_kept, down_found)
    wide_parts = return_rows(jnp.concatenate([both_sum, down_sum], axis=1), place)
    skip = 2 * width - half
    wide_moves = []
    for member in range(plane):
        far_side = member // 2
        down_start = half * (member % 2) + far_side * width
        wide_moves.append(
            [
                (member % 2, half * far_side, 0, half),
                (2, down_start, half + far_side * skip, width - far_side * skip),
            ]
        )
    wgate_grad, wup_grad, wdown_grad = assemble(
        wide_parts, plane_order, wide_moves, [hidden_width] * 3
    )

    late_sum = halving.finish(late_kept, late_found)
    late_parts = return_rows(late_sum, place)
    late_moves = []
    for member in range(plane):
        moves = [(0, member * out_width, 0, out_width)]
        for out, begin, size in (
            (1, 0, query_width),
            (2, query_width, key_width),
            (3, query_width + key_width, key_width),
        ):
            low = max(begin, member * raw_width)
            high = min(begin + size, (member + 1) * raw_width)
            if low < high:
                moves.append((out, low - begin, out_width + low - member * raw_width, high - low))
        late_moves.append(moves)
    wo_grad, wq_grad, wk_grad, wv_grad = assemble(
        late_parts, plane_order, late_moves, [query_width, query_width, key_width, key_width]
    )
    gain_start = out_width + raw_width
    gain_sums = sum(part[:, gain_start : gain_start + 4].astype(f32) for part in late_parts)
    ffngain_grad = gain_sums[:, 0]
    attngain_grad = gain_sums[:, 1]
    head_gains = lax.reduce_precision(gain_sums[:, 2:4], 8, 23)
    head_gains = head_gains + xor_swap(head_gains, "tp", 1)
    if gain_sums.shape[0] < head_dim:
        whole_gains = lax.all_gather(head_gains, everywhere, axis=0, tiled=True)[:head_dim]
    else:
        whole_gains = head_gains[:head_dim]
    return (
        layer_output.reshape(seq_count, block_len, model_width),
        input_grad.reshape(seq_count, block_len, model_width),
        wq_grad,
        wk_grad,
        wv_grad,
        wo_grad,
        wgate_grad,
        wup_grad,
        wdown_grad,
        attngain_grad,
        ffngain_grad,
        whole_gains[:, 0],
        whole_gains[:, 1],
    )


def solution(mesh):
    placed = (
        P("seq", "ctx", None),
        P("seq", "ctx"),
        P(),
        P(),
        P(),
        P(),
        P(None, "tp"),
        P(None, "tp"),
        P(None, "tp"),
        P(None, "tp"),
        P(None, "tp"),
        P(None, "tp"),
        P(None, "tp"),
        P("seq", "ctx", None),
    )
    return jax.shard_map(
        shards,
        mesh=mesh,
        in_specs=placed,
        out_specs=(
            P("seq", "ctx", None),
            P("seq", "ctx", None),
            P(("ctx", "seq"), "tp"),
            P(("ctx", "seq"), "tp"),
            P(("ctx", "seq"), "tp"),
            P(("ctx", "seq"), "tp"),
            P(("ctx", "seq"), "tp"),
            P(("ctx", "seq"), "tp"),
            P(("ctx", "seq"), "tp"),
            P(("ctx", "seq")),
            P(("ctx", "seq")),
            P(),
            P(),
        ),
        check_vma=False,
    )
```

profile of v0, /device:TPU:0, one launch (start us, length us, event | category | flops | bytes accessed | tf_op | source)
XLA Modules:
  0.0 293.0 jit_solution(17461120510881540049)
XLA Ops:
  0.7 4.3 %shard_map.237 = (bf16[4,272,256]{2,1,0:T(8,128)(2,1)}, bf16[256,1024]{1,0:T(8,128)(2,1)}, f32[256,512]{1,0:T(8,128)}, f32[256,256]{1,0:T(8,128)}, f32[256,128]{1,0:T(8,128)}, /*index=5*/f32[256,128]{1,0:T(8,128)}) custom-call(bf16[256,1024]{1,0:T(8,128)(2,1)} %bitcast.108, f32[1,1024]{1,0:T(1,128)} %bitcast.116, bf16[1024,512]{1,0:T(8,128)(2,1)} %refs_10_.1, ...), custom_call_target="tpu_custom_call" | custom-call | flops 536870912 | bytes 4756992 | tf_op jit(solution)/shard_map/pallas_call | solution.py:228
  6.3 3.1 %collective-permute-start = (bf16[272,256]{1,0:T(8,128)(2,1)S(1)}, bf16[272,256]{1,0:T(8,128)(2,1)S(1)}, u32[]{:S(2)}, u32[]{:S(2)}) collective-permute-start(bf16[272,256]{1,0:T(8,128)(2,1)S(1)} %get-tuple-element.102), channel_id=1, source_target_pairs={{0,8},{4,12},{8,0},{12,4},{16,24},{20,28},{24,16},{28,20},{1,9},{5... | collective-permute-start | bytes 417800 | tf_op jit(solution)/shard_map/ppermute | solution.py:37
  16.6 6.1 %collective-permute-done.1.refs_3_ = bf16[272,256]{1,0:T(8,128)(2,1)S(1)} collective-permute-done((bf16[272,256]{1,0:T(8,128)(2,1)S(1)}, bf16[272,256]{1,0:T(8,128)(2,1)S(1)}, u32[]{:S(2)}, u32[]{:S(2)}) %collective-permute-start.1) | collective-permute-done | bytes 139296 | tf_op jit(solution)/shard_map/ppermute | solution.py:37
  29.4 6.2 %shard_map.238 = (bf16[4,256,128]{2,1,0:T(8,128)(2,1)}, f32[8,256]{1,0:T(8,128)}) custom-call(s32[5]{0:T(128)} %pad_add_fusion.2.refs_0_.order_ref, bf16[272,256]{1,0:T(8,128)(2,1)} %copy-done.36, bf16[272,256]{1,0:T(8,128)(2,1)} %copy-done.52, bf16[272,256]{1,0:T(8,128)(2,1)} %copy-done.53, bf16[272,256]{1,0:T(8,128)(2,1)} %copy-done.54, ...), custom_call_target="tpu_custom_call" | custom-call | flops 1073741824 | bytes 1089536 | tf_op jit(solution)/shard_map/pallas_call | solution.py:228
  56.2 13.1 %collective-permute-start.29 = (bf16[256,128]{1,0:T(8,128)(2,1)S(1)}, bf16[256,128]{1,0:T(8,128)(2,1)S(1)}, u32[]{:S(2)}, u32[]{:S(2)}) collective-permute-start(bf16[256,128]{1,0:T(8,128)(2,1)S(1)} %get-tuple-element.115), channel_id=1, source_target_pairs={{0,6},{2,4},{4,2},{6,0},{8,14},{10,12},{12,10},{14,8},{16,22},{18,... | collective-permute-start | bytes 196616 | tf_op jit(solution)/shard_map/ppermute | solution.py:37
  69.8 16.3 %ffn.1 = (f32[256,1024]{1,0:T(8,128)}, bf16[256,1024]{1,0:T(8,128)(2,1)}, bf16[256,2304]{1,0:T(8,128)(2,1)}, bf16[2,2,256,1152]{3,2,1,0:T(8,128)(2,1)}, bf16[256...) custom-call(bf16[256,1024]{1,0:T(8,128)(2,1)} %bitcast.109, bf16[256,1024]{1,0:T(8,128)(2,1)} %get-tuple-element.51.own_ref, ...), custom_call_target="tpu_custom_call" | custom-call | flops 9663676416 | bytes 14155776 | tf_op jit(solution)/shard_map/ffn/pallas_call | solution.py:528
  94.3 4.4 %shard_map.240 = (f32[256,1024]{1,0:T(8,128)}, f32[256,1024]{1,0:T(8,128)}, bf16[256,1024]{1,0:T(8,128)(2,1)}, bf16[4,256,128]{2,1,0:T(8,128)(2,1)}, f32[8,1024]{1,0:T(8,128)}) custom-call(f32[256,1024]{1,0:T(8,128)} %get-tuple-element.52.mixed_ref, bf16[256,1024]{1,0:T(8,128)(2,1)} %get-tuple-element.53.ffn_own_ref, ...), custom_call_target="tpu_custom_call" | custom-call | flops 268435456 | bytes 7639040 | tf_op jit(solution)/shard_map/pallas_call | solution.py:228
  100.3 5.0 %collective-permute-done.44.refs_0_ = bf16[128,1024]{1,0:T(8,128)(2,1)S(1)} collective-permute-done((bf16[128,1024]{1,0:T(8,128)(2,1)S(1)}, bf16[128,1024]{1,0:T(8,128)(2,1)S(1)}, u32[]{:S(2)}, u32[]{:S(2)}) %collective-permute-start.44) | collective-permute-done | bytes 262176 | tf_op jit(solution)/shard_map/ppermute | solution.py:37
  106.0 7.0 %collective-permute-done.46.refs_2_ = bf16[128,1024]{1,0:T(8,128)(2,1)S(1)} collective-permute-done((bf16[128,1024]{1,0:T(8,128)(2,1)S(1)}, bf16[128,1024]{1,0:T(8,128)(2,1)S(1)}, u32[]{:S(2)}, u32[]{:S(2)}) %collective-permute-start.46) | collective-permute-done | bytes 262176 | tf_op jit(solution)/shard_map/ppermute | solution.py:37
  121.9 8.2 %shard_map.241 = (bf16[4,256,128]{2,1,0:T(8,128)(2,1)}, f32[4,256,128]{2,1,0:T(8,128)}, bf16[4,256,128]{2,1,0:T(8,128)(2,1)}) custom-call(s32[5]{0:T(128)} %pad_add_fusion.2.refs_0_.order_ref, bf16[272,256]{1,0:T(8,128)(2,1)} %copy-done.36, bf16[272,256]{1,0:T(8,128)(2,1)} %copy-done.52, bf16[272,256]{1,0:T(8,128)(2,1)} %copy-done.53, ...), custom_call_target="tpu_custom_call" | custom-call | flops 2684354560 | bytes 2400256 | tf_op jit(solution)/shard_map/pallas_call | solution.py:228
  134.9 4.1 %rows.15 = bf16[2,256,640]{2,1,0:T(8,128)(2,1)} custom-call(s32[3]{0:T(128)} %pad_add_fusion.scalars_ref, bf16[256,1024]{1,0:T(8,128)(2,1)} %bitcast.102, bf16[128,2048]{1,0:T(8,128)(2,1)} %copy-done.1, bf16[128,2048]{1,0:T(8,128)(2,1)} %copy-done.2, bf16[128,2048]{1,0:T(8,128)(2,1)} %copy-done.3, bf16[128,2048]{1,0:T(8,128)(2,1)} %copy-done.4, ...), custom_call_target="tpu_custom_call" | custom-call | flops 671088640 | bytes 4718592 | tf_op jit(solution)/shard_map/rows/pallas_call | solution.py:738
  138.9 13.8 %collective-permute-done.16.other_ref = bf16[4,256,128]{2,1,0:T(8,128)(2,1)} collective-permute-done((bf16[4,256,128]{2,1,0:T(8,128)(2,1)}, bf16[4,256,128]{2,1,0:T(8,128)(2,1)}, u32[]{:S(2)}, u32[]{:S(2)}) %collective-permute-start.16) | collective-permute-done | bytes 262176 | tf_op jit(solution)/shard_map/ppermute | solution.py:37
  152.7 4.2 %rows.14 = f32[2,256,640]{2,1,0:T(8,128)} custom-call(s32[3]{0:T(128)} %pad_add_fusion.1.scalars_ref, bf16[256,1024]{1,0:T(8,128)(2,1)} %bitcast.103, bf16[128,2048]{1,0:T(8,128)(2,1)} %copy-done.1, bf16[128,2048]{1,0:T(8,128)(2,1)} %copy-done.2, bf16[128,2048]{1,0:T(8,128)(2,1)} %copy-done.3, bf16[128,2048]{1,0:T(8,128)(2,1)} %copy-done.4, ...), custom_call_target="tpu_custom_call" | custom-call | flops 671088640 | bytes 4718592 | tf_op jit(solution)/shard_map/rows/pallas_call | solution.py:738
  167.8 5.1 %rows.13 = bf16[2,256,1152]{2,1,0:T(8,128)(2,1)} custom-call(s32[3]{0:T(128)} %pad_add_fusion.scalars_ref, bf16[256,1024]{1,0:T(8,128)(2,1)} %get-tuple-element.79.own_ref, bf16[128,1024]{1,0:T(8,128)(2,1)} %copy-done.19, bf16[128,1024]{1,0:T(8,128)(2,1)} %copy-done.20, bf16[128,1024]{1,0:T(8,128)(2,1)} %copy-done.21, ...), custom_call_target="tpu_custom_call" | custom-call | flops 1207959552 | bytes 6815744 | tf_op jit(solution)/shard_map/rows/pallas_call | solution.py:738
  179.8 5.3 %rows.12 = f32[2,256,1152]{2,1,0:T(8,128)} custom-call(s32[3]{0:T(128)} %pad_add_fusion.1.scalars_ref, bf16[256,1024]{1,0:T(8,128)(2,1)} %get-tuple-element.79.own_ref, bf16[128,1024]{1,0:T(8,128)(2,1)} %copy-done.19, bf16[128,1024]{1,0:T(8,128)(2,1)} %copy-done.20, bf16[128,1024]{1,0:T(8,128)(2,1)} %copy-done.21, ...), custom_call_target="tpu_custom_call" | custom-call | flops 1207959552 | bytes 6815744 | tf_op jit(solution)/shard_map/rows/pallas_call | solution.py:738
  185.1 5.4 %shard_map.243 = (bf16[4,256,256]{2,1,0:T(8,128)(2,1)}, bf16[256,1024]{1,0:T(8,128)(2,1)}, f32[8,128]{1,0:T(8,128)}) custom-call(s32[5]{0:T(128)} %pad_add_fusion.2.refs_0_.order_ref, bf16[256,256]{1,0:T(8,128)(2,1)} %get-tuple-element.114.refs_0_, bf16[256,256]{1,0:T(8,128)(2,1)} %copy-done.43, bf16[256,256]{1,0:T(8,128)(2,1)} %copy-done.44, ...), custom_call_target="tpu_custom_call" | custom-call | flops 536870912 | bytes 4723200 | tf_op jit(solution)/shard_map/pallas_call | solution.py:228
  199.9 3.1 %rows.8 = f32[2,256,128]{2,1,0:T(8,128)} custom-call(s32[3]{0:T(128)} %pad_add_fusion.1.scalars_ref, bf16[256,1024]{1,0:T(8,128)(2,1)} %get-tuple-element.68.own_ref, bf16[128,1024]{1,0:T(8,128)(2,1)} %copy-done.27, bf16[128,1024]{1,0:T(8,128)(2,1)} %copy-done.28, bf16[128,1024]{1,0:T(8,128)(2,1)} %collective-permute-done.23.refs_2_, ...), custom_call_target="tpu_custom_call" | custom-call | flops 134217728 | bytes 2621440 | tf_op jit(solution)/shard_map/rows/pallas_call | solution.py:738
  207.0 3.3 %rows.9 = f32[2,256,256]{2,1,0:T(8,128)} custom-call(s32[3]{0:T(128)} %pad_add_fusion.1.scalars_ref, bf16[256,1024]{1,0:T(8,128)(2,1)} %get-tuple-element.70.own_ref, bf16[128,2048]{1,0:T(8,128)(2,1)} %copy-done.1, bf16[128,2048]{1,0:T(8,128)(2,1)} %copy-done.2, bf16[128,2048]{1,0:T(8,128)(2,1)} %copy-done.3, bf16[128,2048]{1,0:T(8,128)(2,1)} %copy-done.4, ...), custom_call_target="tpu_custom_call" | custom-call | flops 268435456 | bytes 3145728 | tf_op jit(solution)/shard_map/rows/pallas_call | solution.py:738
  210.3 3.3 %rows.11 = bf16[2,256,256]{2,1,0:T(8,128)(2,1)} custom-call(s32[3]{0:T(128)} %pad_add_fusion.scalars_ref, bf16[256,1024]{1,0:T(8,128)(2,1)} %get-tuple-element.70.own_ref, bf16[128,2048]{1,0:T(8,128)(2,1)} %copy-done.1, bf16[128,2048]{1,0:T(8,128)(2,1)} %copy-done.2, bf16[128,2048]{1,0:T(8,128)(2,1)} %copy-done.3, bf16[128,2048]{1,0:T(8,128)(2,1)} %copy-done.4, ...), custom_call_target="tpu_custom_call" | custom-call | flops 268435456 | bytes 3145728 | tf_op jit(solution)/shard_map/rows/pallas_call | solution.py:738
  213.5 3.2 %shard_map.244 = (f32[256,1024]{1,0:T(8,128)}, f32[8,1024]{1,0:T(8,128)}) custom-call(bf16[256,1024]{1,0:T(8,128)(2,1)} %bitcast.110, f32[256,1024]{1,0:T(8,128)} %get-tuple-element.56.grad_ref, bf16[256,1024]{1,0:T(8,128)(2,1)} %get-tuple-element.66.own_ref, bf16[256,1024]{1,0:T(8,128)(2,1)} %collective-permute-done.20.other_ref, f32[1,1024]{1,0:T(1,128)} %bitcast.117), custom_call_target="tpu_custom_call" | custom-call | bytes 3706880 | tf_op jit(solution)/shard_map/pallas_call | solution.py:228
  221.7 12.6 %collective-permute-done.39 = bf16[2,256,512]{2,1,0:T(8,128)(2,1)S(1)} collective-permute-done((bf16[2,256,512]{2,1,0:T(8,128)(2,1)S(1)}, bf16[2,256,512]{2,1,0:T(8,128)(2,1)S(1)}, u32[]{:S(2)}, u32[]{:S(2)}) %collective-permute-start.39) | collective-permute-done | bytes 524320 | tf_op jit(solution)/shard_map/ppermute | solution.py:37
  237.7 23.3 %collective-permute-done.40 = bf16[1,256,512]{2,1,0:T(8,128)(2,1)S(1)} collective-permute-done((bf16[1,256,512]{2,1,0:T(8,128)(2,1)S(1)}, bf16[1,256,512]{2,1,0:T(8,128)(2,1)S(1)}, u32[]{:S(2)}, u32[]{:S(2)}) %collective-permute-start.40) | collective-permute-done | bytes 262176 | tf_op jit(solution)/shard_map/ppermute | solution.py:37
  264.7 8.9 %collective-permute-done.54 = bf16[1,256,1152]{2,1,0:T(8,128)(2,1)S(1)} collective-permute-done((bf16[1,256,1152]{2,1,0:T(8,128)(2,1)S(1)}, bf16[1,256,1152]{2,1,0:T(8,128)(2,1)S(1)}, u32[]{:S(2)}, u32[]{:S(2)}) %collective-permute-start.54) | collective-permute-done | bytes 589856 | tf_op jit(solution)/shard_map/ppermute | solution.py:37
  284.8 4.7 %collective-permute-done.62.refs_3_ = bf16[64,1792]{1,0:T(8,128)(2,1)S(1)} collective-permute-done((bf16[64,1792]{1,0:T(8,128)(2,1)S(1)}, bf16[64,1792]{1,0:T(8,128)(2,1)S(1)}, u32[]{:S(2)}, u32[]{:S(2)}) %collective-permute-start.62) | collective-permute-done | bytes 229408 | tf_op jit(solution)/shard_map/ppermute | solution.py:37
  (300 shorter events, 117.7 us)
Async XLA Ops:
  43.1 26.2 %collective-permute-start.31 = (bf16[128,2048]{1,0:T(8,128)(2,1)S(1)}, bf16[128,2048]{1,0:T(8,128)(2,1)S(1)}, u32[]{:S(2)}, u32[]{:S(2)}) collective-permute-start(bf16[128,2048]{1,0:T(8,128)(2,1)S(1)} %pad_maximum_fusion), channel_id=1, source_target_pairs={{0,4},{2,6},{4,0},{6,2},{8,12},{10,14},{12,8},{14,10},{16,20},{18,... | collective-permute-start | bytes 1572872 | tf_op jit(solution)/shard_map/ppermute | solution.py:37
  49.5 19.8 %collective-permute-start.10 = (bf16[256,1024]{1,0:T(8,128)(2,1)}, bf16[256,1024]{1,0:T(8,128)(2,1)}, u32[]{:S(2)}, u32[]{:S(2)}) collective-permute-start(bf16[256,1024]{1,0:T(8,128)(2,1)} %get-tuple-element.51.own_ref), channel_id=1, source_target_pairs={{0,1},{1,0},{2,3},{3,2},{4,5},{5,4},{6,7},{7,6},{8,9},{9,8},{10,11... | collective-permute-start | bytes 1572872 | tf_op jit(solution)/shard_map/ppermute | solution.py:37
  52.6 33.6 %collective-permute-start.32 = (bf16[128,2048]{1,0:T(8,128)(2,1)S(1)}, bf16[128,2048]{1,0:T(8,128)(2,1)S(1)}, u32[]{:S(2)}, u32[]{:S(2)}) collective-permute-start(bf16[128,2048]{1,0:T(8,128)(2,1)S(1)} %pad_maximum_fusion), channel_id=1, source_target_pairs={{0,6},{2,4},{4,2},{6,0},{8,14},{10,12},{12,10},{14,8},{16,22},{18,... | collective-permute-start | bytes 1572872 | tf_op jit(solution)/shard_map/ppermute | solution.py:37
  55.6 30.9 %collective-permute-start.28 = (bf16[256,128]{1,0:T(8,128)(2,1)S(1)}, bf16[256,128]{1,0:T(8,128)(2,1)S(1)}, u32[]{:S(2)}, u32[]{:S(2)}) collective-permute-start(bf16[256,128]{1,0:T(8,128)(2,1)S(1)} %get-tuple-element.116), channel_id=1, source_target_pairs={{0,4},{2,6},{4,0},{6,2},{8,12},{10,14},{12,8},{14,10},{16,20},{18,... | collective-permute-start | bytes 196616 | tf_op jit(solution)/shard_map/ppermute | solution.py:37
  56.2 30.5 %collective-permute-start.29 = (bf16[256,128]{1,0:T(8,128)(2,1)S(1)}, bf16[256,128]{1,0:T(8,128)(2,1)S(1)}, u32[]{:S(2)}, u32[]{:S(2)}) collective-permute-start(bf16[256,128]{1,0:T(8,128)(2,1)S(1)} %get-tuple-element.115), channel_id=1, source_target_pairs={{0,6},{2,4},{4,2},{6,0},{8,14},{10,12},{12,10},{14,8},{16,22},{18,... | collective-permute-start | bytes 196616 | tf_op jit(solution)/shard_map/ppermute | solution.py:37
  69.3 20.1 %collective-permute-start.33 = (bf16[128,2048]{1,0:T(8,128)(2,1)S(1)}, bf16[128,2048]{1,0:T(8,128)(2,1)S(1)}, u32[]{:S(2)}, u32[]{:S(2)}) collective-permute-start(bf16[128,2048]{1,0:T(8,128)(2,1)S(1)} %collective-permute-done.30.refs_0_), channel_id=1, source_target_pairs={{0,1},{1,0},{2,3},{3,2},{4,5},{5,4},{6,7},{7,6},{8,9},{9,8},{10,11... | collective-permute-start | bytes 1572872 | tf_op jit(solution)/shard_map/ppermute | solution.py:37
  69.3 20.2 %collective-permute-start.34 = (bf16[128,2048]{1,0:T(8,128)(2,1)S(1)}, bf16[128,2048]{1,0:T(8,128)(2,1)S(1)}, u32[]{:S(2)}, u32[]{:S(2)}) collective-permute-start(bf16[128,2048]{1,0:T(8,128)(2,1)S(1)} %collective-permute-done.31.refs_1_), channel_id=1, source_target_pairs={{0,1},{1,0},{2,3},{3,2},{4,5},{5,4},{6,7},{7,6},{8,9},{9,8},{10,11... | collective-permute-start | bytes 1572872 | tf_op jit(solution)/shard_map/ppermute | solution.py:37
  89.4 23.6 %collective-permute-start.55 = (bf16[256,640]{1,0:T(8,128)(2,1)}, bf16[256,640]{1,0:T(8,128)(2,1)S(1)}, u32[]{:S(2)}, u32[]{:S(2)}) collective-permute-start(bf16[256,640]{1,0:T(8,128)(2,1)} %get-tuple-element.98), channel_id=1, source_target_pairs={{0,2},{2,0},{4,6},{6,4},{8,10},{10,8},{12,14},{14,12},{16,18},{18,... | collective-permute-start | bytes 983048 | tf_op jit(solution)/shard_map/ppermute | solution.py:37
  89.5 25.6 %collective-permute-start.56 = (bf16[256,640]{1,0:T(8,128)(2,1)}, bf16[256,640]{1,0:T(8,128)(2,1)S(1)}, u32[]{:S(2)}, u32[]{:S(2)}) collective-permute-start(bf16[256,640]{1,0:T(8,128)(2,1)} %get-tuple-element.97), channel_id=1, source_target_pairs={{0,4},{2,6},{4,0},{6,2},{8,12},{10,14},{12,8},{14,10},{16,20},{18,... | collective-permute-start | bytes 983048 | tf_op jit(solution)/shard_map/ppermute | solution.py:37
  93.7 19.3 %collective-permute-start.46 = (bf16[128,1024]{1,0:T(8,128)(2,1)S(1)}, bf16[128,1024]{1,0:T(8,128)(2,1)S(1)}, u32[]{:S(2)}, u32[]{:S(2)}) collective-permute-start(bf16[128,1024]{1,0:T(8,128)(2,1)S(1)} %constant_dynamic-slice_fusion.4), channel_id=1, source_target_pairs={{0,6},{2,4},{4,2},{6,0},{8,14},{10,12},{12,10},{14,8},{16,22},{18,... | collective-permute-start | bytes 786440 | tf_op jit(solution)/shard_map/ppermute | solution.py:37
  105.3 24.9 %collective-permute-start.57 = (bf16[256,640]{1,0:T(8,128)(2,1)}, bf16[256,640]{1,0:T(8,128)(2,1)S(1)}, u32[]{:S(2)}, u32[]{:S(2)}) collective-permute-start(bf16[256,640]{1,0:T(8,128)(2,1)} %get-tuple-element.96), channel_id=1, source_target_pairs={{0,6},{2,4},{4,2},{6,0},{8,14},{10,12},{12,10},{14,8},{16,22},{18,... | collective-permute-start | bytes 983048 | tf_op jit(solution)/shard_map/ppermute | solution.py:37
  106.0 26.9 %collective-permute-start.47 = (bf16[128,1024]{1,0:T(8,128)(2,1)S(1)}, bf16[128,1024]{1,0:T(8,128)(2,1)}, u32[]{:S(2)}, u32[]{:S(2)}) collective-permute-start(bf16[128,1024]{1,0:T(8,128)(2,1)S(1)} %collective-permute-done.44.refs_0_), channel_id=1, source_target_pairs={{0,1},{1,0},{2,3},{3,2},{4,5},{5,4},{6,7},{7,6},{8,9},{9,8},{10,11... | collective-permute-start | bytes 786440 | tf_op jit(solution)/shard_map/ppermute | solution.py:37
  120.5 42.5 %collective-permute-start.50 = (bf16[256,1152]{1,0:T(8,128)(2,1)}, bf16[256,1152]{1,0:T(8,128)(2,1)S(1)}, u32[]{:S(2)}, u32[]{:S(2)}) collective-permute-start(bf16[256,1152]{1,0:T(8,128)(2,1)} %get-tuple-element.91), channel_id=1, source_target_pairs={{0,2},{2,0},{4,6},{6,4},{8,10},{10,8},{12,14},{14,12},{16,18},{18,... | collective-permute-start | bytes 1769480 | tf_op jit(solution)/shard_map/ppermute | solution.py:37
  120.6 42.6 %collective-permute-start.51 = (bf16[256,1152]{1,0:T(8,128)(2,1)}, bf16[256,1152]{1,0:T(8,128)(2,1)S(1)}, u32[]{:S(2)}, u32[]{:S(2)}) collective-permute-start(bf16[256,1152]{1,0:T(8,128)(2,1)} %get-tuple-element.90), channel_id=1, source_target_pairs={{0,4},{2,6},{4,0},{6,2},{8,12},{10,14},{12,8},{14,10},{16,20},{18,... | collective-permute-start | bytes 1769480 | tf_op jit(solution)/shard_map/ppermute | solution.py:37
  130.1 36.8 %collective-permute-start.52 = (bf16[256,1152]{1,0:T(8,128)(2,1)}, bf16[256,1152]{1,0:T(8,128)(2,1)S(1)}, u32[]{:S(2)}, u32[]{:S(2)}) collective-permute-start(bf16[256,1152]{1,0:T(8,128)(2,1)} %get-tuple-element.89), channel_id=1, source_target_pairs={{0,6},{2,4},{4,2},{6,0},{8,14},{10,12},{12,10},{14,8},{16,22},{18,... | collective-permute-start | bytes 1769480 | tf_op jit(solution)/shard_map/ppermute | solution.py:37
  132.9 19.8 %collective-permute-start.16 = (bf16[4,256,128]{2,1,0:T(8,128)(2,1)}, bf16[4,256,128]{2,1,0:T(8,128)(2,1)}, u32[]{:S(2)}, u32[]{:S(2)}) collective-permute-start(bf16[4,256,128]{2,1,0:T(8,128)(2,1)} %get-tuple-element.61), channel_id=1, source_target_pairs={{0,4},{4,0},{8,12},{12,8},{16,20},{20,16},{24,28},{28,24},{1,5},{5... | collective-permute-start | bytes 786440 | tf_op jit(solution)/shard_map/ppermute | solution.py:37
  134.2 26.8 %collective-permute-start.49 = (bf16[128,1024]{1,0:T(8,128)(2,1)S(1)}, bf16[128,1024]{1,0:T(8,128)(2,1)S(1)}, u32[]{:S(2)}, u32[]{:S(2)}) collective-permute-start(bf16[128,1024]{1,0:T(8,128)(2,1)S(1)} %copy-done.22), channel_id=1, source_target_pairs={{0,1},{1,0},{2,3},{3,2},{4,5},{5,4},{6,7},{7,6},{8,9},{9,8},{10,11... | collective-permute-start | bytes 786440 | tf_op jit(solution)/shard_map/ppermute | solution.py:37
  152.7 41.3 %collective-permute-start.58 = (bf16[2,256,640]{2,1,0:T(8,128)(2,1)}, bf16[2,256,640]{2,1,0:T(8,128)(2,1)}, u32[]{:S(2)}, u32[]{:S(2)}) collective-permute-start(bf16[2,256,640]{2,1,0:T(8,128)(2,1)} %rows.15), channel_id=1, source_target_pairs={{0,8},{2,10},{4,12},{6,14},{8,0},{10,2},{12,4},{14,6},{16,24},{18,... | collective-permute-start | bytes 1966088 | tf_op jit(solution)/shard_map/ppermute | solution.py:37
  166.9 23.6 %collective-permute-start.21 = (bf16[128,1024]{1,0:T(8,128)(2,1)}, bf16[128,1024]{1,0:T(8,128)(2,1)S(1)}, u32[]{:S(2)}, u32[]{:S(2)}) collective-permute-start(bf16[128,1024]{1,0:T(8,128)(2,1)} %constant_dynamic-slice_fusion.7), channel_id=1, source_target_pairs={{0,2},{2,0},{4,6},{6,4},{8,10},{10,8},{12,14},{14,12},{16,18},{18,... | collective-permute-start | bytes 786440 | tf_op jit(solution)/shard_map/ppermute | solution.py:37
  179.8 40.3 %collective-permute-start.53 = (bf16[2,256,1152]{2,1,0:T(8,128)(2,1)}, bf16[2,256,1152]{2,1,0:T(8,128)(2,1)}, u32[]{:S(2)}, u32[]{:S(2)}) collective-permute-start(bf16[2,256,1152]{2,1,0:T(8,128)(2,1)} %rows.13), channel_id=1, source_target_pairs={{0,8},{2,10},{4,12},{6,14},{8,0},{10,2},{12,4},{14,6},{16,24},{18,... | collective-permute-start | bytes 3538952 | tf_op jit(solution)/shard_map/ppermute | solution.py:37
  190.5 23.0 %collective-permute-start.20 = (bf16[256,1024]{1,0:T(8,128)(2,1)}, bf16[256,1024]{1,0:T(8,128)(2,1)}, u32[]{:S(2)}, u32[]{:S(2)}) collective-permute-start(bf16[256,1024]{1,0:T(8,128)(2,1)} %get-tuple-element.66.own_ref), channel_id=1, source_target_pairs={{0,1},{1,0},{2,3},{3,2},{4,5},{5,4},{6,7},{7,6},{8,9},{9,8},{10,11... | collective-permute-start | bytes 1572872 | tf_op jit(solution)/shard_map/ppermute | solution.py:37
  206.2 31.4 %collective-permute-start.59 = (bf16[1,256,640]{2,1,0:T(8,128)(2,1)S(1)}, bf16[1,256,640]{2,1,0:T(8,128)(2,1)S(1)}, u32[]{:S(2)}, u32[]{:S(2)}) collective-permute-start(bf16[1,256,640]{2,1,0:T(8,128)(2,1)S(1)} %dynamic-slice_convert_fusion.1), channel_id=1, source_target_pairs={{0,16},{2,18},{4,20},{6,22},{8,24},{10,26},{12,28},{14,30},{16,0},... | collective-permute-start | bytes 983048 | tf_op jit(solution)/shard_map/ppermute | solution.py:37
  234.5 26.5 %collective-permute-start.40 = (bf16[1,256,512]{2,1,0:T(8,128)(2,1)S(1)}, bf16[1,256,512]{2,1,0:T(8,128)(2,1)S(1)}, u32[]{:S(2)}, u32[]{:S(2)}) collective-permute-start(bf16[1,256,512]{2,1,0:T(8,128)(2,1)S(1)} %dynamic-slice_convert_fusion.2), channel_id=1, source_target_pairs={{0,16},{2,18},{4,20},{6,22},{8,24},{10,26},{12,28},{14,30},{16,0},... | collective-permute-start | bytes 786440 | tf_op jit(solution)/shard_map/ppermute | solution.py:37
  234.7 38.9 %collective-permute-start.54 = (bf16[1,256,1152]{2,1,0:T(8,128)(2,1)S(1)}, bf16[1,256,1152]{2,1,0:T(8,128)(2,1)S(1)}, u32[]{:S(2)}, u32[]{:S(2)}) collective-permute-start(bf16[1,256,1152]{2,1,0:T(8,128)(2,1)S(1)} %dynamic-slice_convert_fusion), channel_id=1, source_target_pairs={{0,16},{2,18},{4,20},{6,22},{8,24},{10,26},{12,28},{14,30},{16,0},... | collective-permute-start | bytes 1769480 | tf_op jit(solution)/shard_map/ppermute | solution.py:37
  (102 other events, 792.0 us)
where the time goes:
time: 294 us; the launch traced here: 293 us
  waiting for transfers between devices  96.8 us (33%)
  Pallas kernels  89 us (30%)
  starting transfers between devices  74.4 us (25%)
  local copies, waits for them, and re-layouts  24.7 us (8%)
  other arithmetic  6.66 us (2%)
    ppermute x64, waiting for transfers between devices, xor_swap(): lax.ppermute(value, axis, [(index, index ^ flip) for index in range(size)])  96.8 us
    ppermute x64, starting transfers between devices, xor_swap(): lax.ppermute(value, axis, [(index, index ^ flip) for index in range(size)])  74.4 us
    pallas_call x10, Pallas kernels, whole_call(): pl.pallas_call(kernel, out_shape=tuple(outs), in_specs=[smem_spec()] * le...  41.3 us
    pallas_call x8, Pallas kernels, rows_call(): pl.pallas_call(rows_kernel, grid=(steps,), out_shape=shape_of((steps, hei...  31.4 us
    pallas_call x1, Pallas kernels, ffn_call(): pl.pallas_call(functools.partial(ffn_kernel, steps), grid=(steps,), out_s...  16.3 us
    squeeze x9, local copies, waits for them, and re-layouts, pick(): return lax.dynamic_index_in_dim(value, index, axis, keepdims=False)  12.8 us
  transfers between devices with their start and end apart: 64, of which 17 were waited for; matrix products, arithmetic and copies ran while one was open for 8% of the time, Pallas kernels for 26%

commit v1 on v0

v1 whole, which is shorter than its diff:
```python
import functools
import math

import jax
import jax.numpy as jnp
from jax import lax
from jax.experimental import pallas as pl
from jax.experimental.pallas import tpu as pltpu
from jax.sharding import PartitionSpec as P


eps_norm = 1e-05
theta_base = 1000000.0
negative = -1e30
bf16 = jnp.bfloat16
f32 = jnp.float32
lanes = 128
pos_shift = 7
pos_base = 1 << pos_shift
pos_rows = 16
ffn_tile = 256
vmem_limit = 28 * 1024 * 1024


def dot_f32(lhs, rhs, lhs_dim, rhs_dim):
    return lax.dot_general(
        lhs, rhs, (((lhs_dim,), (rhs_dim,)), ((), ())), preferred_element_type=f32
    )


def rms_back(grad_in, values, stat_val):
    return stat_val * grad_in - values * stat_val**3 * jnp.mean(
        grad_in * values, axis=-1, keepdims=True
    )


def xor_swap(value, axis, flip):
    size = lax.axis_size(axis)
    return lax.ppermute(value, axis, [(index, index ^ flip) for index in range(size)])


def named_swap(value, axis="tp"):
    return xor_swap(value, axis, 1)


def level_swap(parts):
    count = len(parts)
    found = [parts[0]] + [None] * (count - 1)
    for flip in range(count - 1, 0, -1):
        found[flip] = xor_swap(parts[flip], "ctx", 2 * flip)
    return found


def side_swap(parts):
    return [xor_swap(part, "ctx", 1) for part in parts]


def plane_swap(parts):
    return [parts[0]] + [
        xor_swap(parts[flip], everywhere, flip) for flip in range(1, len(parts))
    ]


everywhere = ("ctx", "seq")
plane = 4
at_level, at_side, at_core, at_place, at_bits = range(5)


def fill_heads(ref, place, rows, head_dim):
    tokens_count = rows.shape[0]
    for head in range(rows.shape[1] // head_dim):
        ref[place, head * tokens_count : (head + 1) * tokens_count, :] = rows[
            :, head * head_dim : (head + 1) * head_dim
        ]


def gather_blocks(
    info_ref, block_refs, own_refs, other_refs, query_buf, key_buf, value_buf, low_buf
):
    count = len(block_refs)
    seq_count = key_buf.shape[0]
    head_dim = key_buf.shape[2]
    block_len = own_refs[0].shape[0] // seq_count
    side = info_ref[at_side]
    for flip in range(count):
        level = info_ref[at_level] ^ flip
        block_ref = block_refs[flip]
        own_start = pl.multiple_of((level * 2 + side) * block_len, block_len)
        other_start = pl.multiple_of((level * 2 + 1 - side) * block_len, block_len)
        tail = block_ref[seq_count * block_len :, :].astype(f32)
        found = tail[:seq_count] * pos_base + tail[seq_count : 2 * seq_count]
        token = own_start + lax.broadcasted_iota(jnp.int32, (1, block_len), 1)
        for seq in range(seq_count):
            part = slice(seq * block_len, (seq + 1) * block_len)
            fill_heads(query_buf, seq * count + level, block_ref[part, :], head_dim)
            for refs, start in ((own_refs, own_start), (other_refs, other_start)):
                rows = pl.ds(start, block_len)
                key_buf[seq, rows, :] = refs[flip][part, :head_dim]
                value_buf[seq, rows, :] = refs[flip][part, head_dim:]
            low_buf[seq * count + level] = token - found[seq : seq + 1].astype(jnp.int32)


def visible(info_ref, low_row, level, key_count, block_len, width):
    low = jnp.concatenate([low_row] * (width // block_len), axis=1)
    shape = (key_count, low.shape[1])
    key_index = lax.broadcasted_iota(jnp.int32, shape, 0)
    lane = lax.broadcasted_iota(jnp.int32, shape, 1) % block_len
    query_index = (level * 2 + info_ref[at_side]) * block_len + lane
    return (key_index <= query_index) & (key_index >= low)


def unfold(turned, block_len):
    parts = [
        turned[:, start : start + block_len] for start in range(0, turned.shape[1], block_len)
    ]
    return jnp.concatenate(parts, axis=0).T


def attend_kernel(count, *refs):
    info_ref = refs[0]
    sources = [refs[1 + n * count : 1 + (n + 1) * count] for n in range(3)]
    out_ref, lse_ref = refs[1 + 3 * count : 3 + 3 * count]
    send_refs = refs[3 + 3 * count : 3 + 4 * count]
    query_buf, key_buf, value_buf, low_buf = refs[3 + 4 * count :]
    gather_blocks(info_ref, *sources, query_buf, key_buf, value_buf, low_buf)
    seq_count, _, head_dim = key_buf.shape
    block_len = low_buf.shape[2]
    for seq in range(seq_count):
        for level in range(count):
            place = seq * count + level
            key_count = 2 * block_len * (level + 1)
            query = query_buf[place]
            scores = dot_f32(key_buf[seq, :key_count, :], query, 1, 1) * head_dim ** (-0.5)
            allowed = visible(info_ref, low_buf[place], level, key_count, block_len, query.shape[0])
            scores = jnp.where(allowed, scores, negative)
            top = jnp.max(scores, axis=0, keepdims=True)
            weights = jnp.exp(scores - top)
            row_sum = jnp.sum(weights, axis=0, keepdims=True)
            lse_ref[place : place + 1, :] = top + jnp.log(row_sum)
            turned = dot_f32(value_buf[seq, :key_count, :], weights.astype(bf16), 0, 0) / row_sum
            out_ref[level, seq * block_len : (seq + 1) * block_len, :] = unfold(
                turned, block_len
            ).astype(bf16)
    for flip in range(count):
        send_refs[flip][...] = out_ref[info_ref[at_level] ^ flip]


def attend_back_kernel(count, *refs):
    info_ref = refs[0]
    sources = [refs[1 + n * count : 1 + (n + 1) * count] for n in range(3)]
    grad_refs = refs[1 + 3 * count : 1 + 4 * count]
    out_ref, lse_ref = refs[1 + 4 * count : 3 + 4 * count]
    query_refs = refs[3 + 4 * count : 3 + 5 * count]
    own_refs = refs[3 + 5 * count : 3 + 6 * count]
    other_refs = refs[3 + 6 * count : 3 + 7 * count]
    (
        query_buf,
        key_buf,
        value_buf,
        low_buf,
        grad_buf,
        key_acc,
        value_acc,
        query_grad,
    ) = refs[3 + 7 * count :]
    gather_blocks(info_ref, *sources, query_buf, key_buf, value_buf, low_buf)
    seq_count, _, head_dim = key_buf.shape
    block_len = low_buf.shape[2]
    group = lanes // head_dim
    for flip in range(count):
        for seq in range(seq_count):
            rows = grad_refs[flip][seq * block_len : (seq + 1) * block_len, :]
            level = info_ref[at_level] ^ flip
            fill_heads(grad_buf, seq * count + level, rows, head_dim)
    key_acc[...] = jnp.zeros_like(key_acc)
    value_acc[...] = jnp.zeros_like(value_acc)
    scale = head_dim ** (-0.5)
    ones_row = jnp.ones((8, head_dim), f32)
    for seq in range(seq_count):
        for level in range(count):
            place = seq * count + level
            key_count = 2 * block_len * (level + 1)
            keys = key_buf[seq, :key_count, :]
            query = query_buf[place]
            grad = grad_buf[place]
            rows = out_ref[level, seq * block_len : (seq + 1) * block_len, :]
            out = jnp.concatenate(
                [rows[:, head * head_dim : (head + 1) * head_dim] for head in range(group)], axis=0
            )
            delta = lax.dot_general(
                ones_row,
                grad.astype(f32) * out.astype(f32),
                (((1,), (1,)), ((), ())),
                precision=lax.Precision.HIGHEST,
                preferred_element_type=f32,
            )[:1, :]
            scores = dot_f32(keys, query, 1, 1) * scale
            allowed = visible(info_ref, low_buf[place], level, key_count, block_len, query.shape[0])
            probs = jnp.where(allowed, jnp.exp(scores - lse_ref[place : place + 1, :]), 0.0)
            grad_probs = dot_f32(value_buf[seq, :key_count, :], grad, 1, 1)
            grad_scores = (probs * (grad_probs - delta)).astype(bf16)
            value_acc[seq, :key_count, :] += dot_f32(probs.astype(bf16), grad, 1, 0)
            key_acc[seq, :key_count, :] += dot_f32(grad_scores, query, 1, 0)
            turned = dot_f32(keys, grad_scores, 0, 0) * scale
            query_grad[level, seq * block_len : (seq + 1) * block_len, :] = unfold(
                turned, block_len
            ).astype(bf16)
    side = info_ref[at_side]
    for flip in range(count):
        level = info_ref[at_level] ^ flip
        query_refs[flip][...] = query_grad[level]
        for seq in range(seq_count):
            part = slice(seq * block_len, (seq + 1) * block_len)
            for place, ref in ((side, own_refs[flip]), (1 - side, other_refs[flip])):
                start = pl.multiple_of((2 * level + place) * block_len, block_len)
                rows = pl.ds(start, block_len)
                both = [key_acc[seq, rows, :] * scale, value_acc[seq, rows, :]]
                ref[part, :] = jnp.concatenate(both, axis=1).astype(ref.dtype)


def merge_kernel(count, *refs):
    for flip in range(count):
        own_ref, other_ref, out_ref = refs[flip::count]
        out_ref[...] = (own_ref[...] + other_ref[...].astype(f32)).astype(bf16)


def smem_spec():
    return pl.BlockSpec(memory_space=pltpu.SMEM)


def vmem_spec():
    return pl.BlockSpec(memory_space=pltpu.VMEM)


def shape_of(shape, dtype):
    return jax.ShapeDtypeStruct(shape, dtype)


def whole_call(kernel, outs, args, scalars=(), scratch=(), flops=0):
    moved = sum(arg.size * arg.dtype.itemsize for arg in args)
    moved += sum(out.size * jnp.dtype(out.dtype).itemsize for out in outs)
    return pl.pallas_call(
        kernel,
        out_shape=tuple(outs),
        in_specs=[smem_spec()] * len(scalars) + [vmem_spec()] * len(args),
        out_specs=tuple(vmem_spec() for _ in outs),
        scratch_shapes=list(scratch),
        cost_estimate=pl.CostEstimate(flops=flops, bytes_accessed=moved, transcendentals=0),
        compiler_params=pltpu.CompilerParams(vmem_limit_bytes=vmem_limit),
    )(*scalars, *args)


def head_scratch(seq_count, count, block_len, head_dim):
    total = 2 * count * block_len
    heads_rows = lanes // head_dim * block_len
    return [
        pltpu.VMEM((seq_count * count, heads_rows, head_dim), bf16),
        pltpu.VMEM((seq_count, total, head_dim), bf16),
        pltpu.VMEM((seq_count, total, head_dim), bf16),
        pltpu.VMEM((seq_count * count, 1, block_len), jnp.int32),
    ]


def head_forward(info, sources, seq_count, head_dim):
    count = len(sources) // 3
    row_count = sources[-1].shape[0]
    block_len = row_count // seq_count
    heads_rows = lanes // head_dim * block_len
    found = whole_call(
        functools.partial(attend_kernel, count),
        [
            shape_of((count, row_count, lanes), bf16),
            shape_of((seq_count * count, heads_rows), f32),
        ]
        + [shape_of((row_count, lanes), bf16)] * count,
        sources,
        scalars=(info,),
        scratch=head_scratch(seq_count, count, block_len, head_dim),
        flops=8 * row_count * row_count * count * count * lanes,
    )
    return (found[0], found[1], found[2:])


def head_backward(info, sources, grads, out, log_sum, seq_count, head_dim):
    count = len(sources) // 3
    row_count = sources[-1].shape[0]
    block_len = row_count // seq_count
    heads_rows = lanes // head_dim * block_len
    total = 2 * count * block_len
    found = whole_call(
        functools.partial(attend_back_kernel, count),
        [shape_of((row_count, lanes), bf16)] * count
        + [shape_of((row_count, lanes), f32)] * count
        + [shape_of((row_count, lanes), bf16)] * count,
        [*sources, *grads, out, log_sum],
        scalars=(info,),
        scratch=head_scratch(seq_count, count, block_len, head_dim)
        + [
            pltpu.VMEM((seq_count * count, heads_rows, head_dim), bf16),
            pltpu.VMEM((seq_count, total, head_dim), f32),
            pltpu.VMEM((seq_count, total, head_dim), f32),
            pltpu.VMEM((count, row_count, lanes), bf16),
        ],
        flops=20 * row_count * row_count * count * count * lanes,
    )
    return (found[:count], found[count : 2 * count], found[2 * count :])


def gathered_scores(query_grouped, key_piece, query_pos, lowest_pos, key_pos):
    head_dim = query_grouped.shape[-1]
    keys_split = key_piece.reshape(
        key_piece.shape[0], key_piece.shape[1], query_grouped.shape[2], head_dim
    )
    scores = jnp.einsum(
        "sqhgd,skhd->shgqk", query_grouped, keys_split, preferred_element_type=f32
    ) * head_dim ** (-0.5)
    allowed = (key_pos[None, None, :] <= query_pos[None, :, None]) & (
        key_pos[None, None, :] >= lowest_pos[:, :, None]
    )
    allowed = allowed[:, None, None, :, :]
    return (jnp.where(allowed, scores, negative), allowed, keys_split)


def gathered_forward(query_grouped, key_rows, value_rows, query_index, lowest_key):
    key_all = lax.all_gather(key_rows, "ctx", axis=1, tiled=True)
    value_all = lax.all_gather(value_rows, "ctx", axis=1, tiled=True)
    key_pos = jnp.arange(key_all.shape[1], dtype=jnp.int32)
    scores, allowed, keys_split = gathered_scores(
        query_grouped, key_all, query_index, lowest_key, key_pos
    )
    top = jnp.max(scores, axis=-1)
    weights = jnp.where(allowed, jnp.exp(scores - top[..., None]), 0.0)
    row_sum = jnp.sum(weights, axis=-1)
    summed = jnp.einsum(
        "shgqk,skhd->shgqd",
        weights.astype(bf16),
        value_all.reshape(keys_split.shape),
        preferred_element_type=f32,
    )
    attended = (summed / row_sum[..., None]).astype(bf16)
    return (jnp.transpose(attended, (0, 3, 1, 2, 4)), top + jnp.log(row_sum), key_all, value_all)


def gathered_backward(
    query_grouped, grad_grouped, attended, log_sum, key_all, value_all, query_index, lowest_key
):
    scale = query_grouped.shape[-1] ** (-0.5)
    key_pos = jnp.arange(key_all.shape[1], dtype=jnp.int32)
    delta_rows = jnp.sum(grad_grouped.astype(f32) * attended.astype(f32), axis=-1)
    delta_stat = jnp.transpose(delta_rows, (0, 2, 3, 1))
    scores, allowed, keys_split = gathered_scores(
        query_grouped, key_all, query_index, lowest_key, key_pos
    )
    probs = jnp.where(allowed, jnp.exp(scores - log_sum[..., None]), 0.0)
    grad_probs = jnp.einsum(
        "sqhgd,skhd->shgqk",
        grad_grouped,
        value_all.reshape(keys_split.shape),
        preferred_element_type=f32,
    )
    grad_scores = (probs * (grad_probs - delta_stat[..., None])).astype(bf16)
    query_grad = (
        jnp.einsum("shgqk,skhd->sqhgd", grad_scores, keys_split, preferred_element_type=f32) * scale
    )
    key_grad = (
        jnp.einsum("shgqk,sqhgd->skhd", grad_scores, query_grouped, preferred_element_type=f32)
        * scale
    )
    value_grad = jnp.einsum(
        "shgqk,sqhgd->skhd", probs.astype(bf16), grad_grouped, preferred_element_type=f32
    )
    key_own, value_own = (
        lax.psum_scatter(part.reshape(key_all.shape), "ctx", scatter_dimension=1, tiled=True)
        for part in (key_grad, value_grad)
    )
    return (query_grad, key_own, value_own)


def split_dot(value, table):
    high = value.astype(bf16)
    low = (value - high.astype(f32)).astype(bf16)
    return dot_f32(high, table, 1, 0) + dot_f32(low, table, 1, 0)


def head_table(head_dim):
    row = lax.broadcasted_iota(jnp.int32, (lanes, lanes), 0) // head_dim
    col = lax.broadcasted_iota(jnp.int32, (lanes, lanes), 1) // head_dim
    return jnp.where(row == col, 1.0 / head_dim, 0.0).astype(bf16)


def swap_halves(value, head_dim):
    lane = lax.broadcasted_iota(jnp.int32, value.shape, 1)
    ahead = pltpu.roll(value, lanes - head_dim // 2, 1)
    behind = pltpu.roll(value, head_dim // 2, 1)
    return jnp.where(lane % head_dim < head_dim // 2, ahead, behind)


def front_kernel(
    head_dim,
    info_ref,
    tokens_ref,
    cot_ref,
    gain_ref,
    query_w_ref,
    key_w_ref,
    value_w_ref,
    q_gain_ref,
    k_gain_ref,
    pos_ref,
    normed_ref,
    early_ref,
    query_ref,
    key_ref,
    cos_ref,
    sin_ref,
    *refs,
):
    count = (len(refs) - 2) // 2
    block_refs = refs[:count]
    pair_refs = refs[count : 2 * count]
    blocks_ref, pairs_ref = refs[2 * count :]
    seq_count, block_len = pos_ref.shape
    half_dim = head_dim // 2
    places = pos_ref[...]
    spare = jnp.zeros((8 - seq_count, block_len), f32)
    columns = jnp.concatenate([places.astype(f32), spare], axis=0).T
    lane_row = lax.broadcasted_iota(jnp.int32, (1, lanes), 1)
    exponent = (lane_row % half_dim).astype(f32) * (-2.0 / head_dim)
    frequency = jnp.exp(exponent * math.log(theta_base))
    sign = jnp.where(lane_row % head_dim < half_dim, -1.0, 1.0)
    for seq in range(seq_count):
        angles = columns[:, seq : seq + 1] * frequency
        cos_ref[seq * block_len : (seq + 1) * block_len, :] = jnp.cos(angles)
        sin_ref[seq * block_len : (seq + 1) * block_len, :] = jnp.sin(angles) * sign
    packed_pos = jnp.concatenate([places >> pos_shift, places & (pos_base - 1)], axis=0).astype(f32)
    fill = jnp.zeros((pos_rows - 2 * seq_count, block_len), f32)
    pos_tail = jnp.concatenate([packed_pos, fill], axis=0).astype(bf16)
    q_gain_row = jnp.concatenate([q_gain_ref[...]] * (lanes // head_dim), axis=1)
    k_gain_row = jnp.concatenate([k_gain_ref[...]] * (lanes // head_dim), axis=1)
    rows = tokens_ref[...].astype(f32)
    stat = lax.rsqrt(jnp.mean(rows * rows, axis=1, keepdims=True) + eps_norm)
    normed = (rows * stat * gain_ref[...]).astype(bf16)
    normed_ref[...] = normed
    half = rows.shape[0] // 2
    model_width = rows.shape[1]
    half_rows = pl.ds(pl.multiple_of(info_ref[at_core] * half, half), half)
    early_ref[:, :model_width] = cot_ref[half_rows, :]
    early_ref[:, model_width:] = normed_ref[half_rows, :]
    query = dot_f32(normed, query_w_ref[...], 1, 0)
    key = dot_f32(normed, key_w_ref[...], 1, 0)
    value = dot_f32(normed, value_w_ref[...], 1, 0).astype(bf16).astype(f32)
    query_ref[...] = query
    key_ref[...] = key
    table = head_table(head_dim)
    cosine = cos_ref[...]
    sine = sin_ref[...]
    kv_heads = key.shape[1] // head_dim
    lane = lax.broadcasted_iota(jnp.int32, (rows.shape[0], lanes), 1)

    def turned(tile, gain):
        stat_val = lax.rsqrt(split_dot(tile * tile, table) + eps_norm)
        scaled = tile * stat_val * gain
        return scaled * cosine + swap_halves(scaled, head_dim) * sine

    for head in range(kv_heads):
        query_tile = turned(query[:, head * lanes : (head + 1) * lanes], q_gain_row).astype(bf16)
        pair = slice(head // 2 * lanes, (head // 2 + 1) * lanes)
        key_tile = turned(key[:, pair], k_gain_row)
        value_tile = value[:, pair]
        if head % 2 == 0:
            value_tile = pltpu.roll(value_tile, head_dim, 1)
        else:
            key_tile = pltpu.roll(key_tile, head_dim, 1)
        both = jnp.where(lane < head_dim, key_tile, value_tile).astype(bf16)
        row_count = rows.shape[0]
        blocks_ref[head, :row_count, :] = query_tile
        blocks_ref[head, row_count:, :] = pos_tail
        pairs_ref[head] = both
    for flip in range(count):
        head = info_ref[at_level] ^ flip
        block_refs[flip][...] = blocks_ref[head]
        pair_refs[flip][...] = pairs_ref[head]


def project_kernel(info_ref, *refs):
    count = (len(refs) - 3) // 2
    block_refs = refs[:count]
    weight_ref, part_ref = refs[count : count + 2]
    send_refs = refs[count + 2 : 2 * count + 2]
    heads_ref = refs[2 * count + 2]
    for flip in range(count):
        heads_ref[info_ref[at_level] ^ flip] = block_refs[flip][...]
    total = None
    for head in range(count):
        found = dot_f32(heads_ref[head], weight_ref[:, head * lanes : (head + 1) * lanes], 1, 1)
        total = found if total is None else total + found
    part_ref[...] = total.astype(bf16)
    for flip in range(plane):
        send_refs[flip][...] = heads_ref[info_ref[at_place] ^ flip]


def ffn_kernel(
    steps,
    info_ref,
    tokens_ref,
    own_ref,
    other_ref,
    gain_ref,
    cot_ref,
    gate_ref,
    up_ref,
    down_ref,
    mixed_ref,
    normed_ref,
    half_ref,
    ffn_ref,
    back_ref,
    *refs,
):
    hidden_refs = refs[:plane]
    both_refs = refs[plane : 2 * plane]
    ffn_acc, back_acc, hidden_buf, gate_buf, up_buf = refs[2 * plane :]
    step = pl.program_id(0)
    tile = gate_ref.shape[1]
    width = hidden_refs[0].shape[1]
    half = steps * tile // 2

    @pl.when(step == 0)
    def _():
        mixed = tokens_ref[...].astype(f32) + (own_ref[...].astype(f32) + other_ref[...].astype(f32))
        mixed_ref[...] = mixed
        stat = lax.rsqrt(jnp.mean(mixed * mixed, axis=1, keepdims=True) + eps_norm)
        normed_ref[...] = (mixed * stat * gain_ref[...]).astype(bf16)
        half_count = half_ref.shape[0]
        start = pl.multiple_of(info_ref[at_core] * half_count, half_count)
        half_ref[...] = normed_ref[pl.ds(start, half_count), :]
        ffn_acc[...] = jnp.zeros_like(ffn_acc)
        back_acc[...] = jnp.zeros_like(back_acc)

    normed = normed_ref[...]
    gate = dot_f32(normed, gate_ref[...], 1, 0)
    up = dot_f32(normed, up_ref[...], 1, 0)
    grad = dot_f32(cot_ref[...], down_ref[...], 1, 0)
    sig = jax.nn.sigmoid(gate)
    silu = gate * sig
    hidden = (silu * up).astype(bf16)
    cols = pl.ds(pl.multiple_of(step * tile, tile), tile)
    hidden_buf[:, cols] = hidden
    grad_gate = (grad * up * (sig * (1.0 + gate * (1.0 - sig)))).astype(bf16)
    grad_up = (grad * silu).astype(bf16)
    gate_buf[:, cols] = grad_gate
    up_buf[:, cols] = grad_up
    ffn_acc[...] += dot_f32(hidden, down_ref[...], 1, 1)
    back_acc[...] += dot_f32(grad_gate, gate_ref[...], 1, 1) + dot_f32(grad_up, up_ref[...], 1, 1)

    @pl.when(step == steps - 1)
    def _():
        ffn_ref[...] = ffn_acc[...].astype(bf16)
        back_ref[...] = back_acc[...].astype(bf16)
        for flip in range(plane):
            member = info_ref[at_place] ^ flip
            start = (member % 2) * half + (member // 2) * (half - width)
            hidden_refs[flip][...] = hidden_buf[:, pl.ds(pl.multiple_of(start, lanes), width)]
            side = pl.ds(pl.multiple_of(member // 2 * half, lanes), half)

            @pl.when(member % 2 == 0)
            def _():
                both_refs[flip][...] = gate_buf[:, side]

            @pl.when(member % 2 == 1)
            def _():
                both_refs[flip][...] = up_buf[:, side]


def ffn_call(info, tokens_in, own, other, gain, cot, w_gate, w_up, w_down):
    row_count, model_width = tokens_in.shape
    cols = w_gate.shape[1]
    half, width = window(cols)
    tile = ffn_tile
    steps = cols // tile
    fixed = lambda *shape: pl.BlockSpec(shape, lambda step, info_ref: (0,) * len(shape))
    moving = pl.BlockSpec((model_width, tile), lambda step, info_ref: (0, step))
    rows_spec = fixed(row_count, model_width)
    wide = (row_count, model_width)
    found = pl.pallas_call(
        functools.partial(ffn_kernel, steps),
        grid_spec=pltpu.PrefetchScalarGridSpec(
            num_scalar_prefetch=1,
            grid=(steps,),
            in_specs=[rows_spec, rows_spec, rows_spec, fixed(1, model_width), rows_spec]
            + [moving] * 3,
            out_specs=[rows_spec, rows_spec, fixed(row_count // 2, model_width)]
            + [rows_spec] * 2
            + [fixed(row_count, width)] * plane
            + [fixed(row_count, half)] * plane,
            scratch_shapes=[pltpu.VMEM(wide, f32), pltpu.VMEM(wide, f32)]
            + [pltpu.VMEM((row_count, cols), bf16)] * 3,
        ),
        out_shape=[
            shape_of(wide, f32),
            shape_of(wide, bf16),
            shape_of((row_count // 2, model_width), bf16),
            shape_of(wide, bf16),
            shape_of(wide, bf16),
        ]
        + [shape_of((row_count, width), bf16)] * plane
        + [shape_of((row_count, half), bf16)] * plane,
        cost_estimate=pl.CostEstimate(
            flops=16 * row_count * model_width * cols,
            bytes_accessed=6 * model_width * cols,
            transcendentals=row_count * cols,
        ),
        compiler_params=pltpu.CompilerParams(vmem_limit_bytes=vmem_limit),
        name="ffn",
    )(info, tokens_in, own, other, gain, cot, w_gate, w_up, w_down)
    return (*found[:5], found[5 : 5 + plane], found[5 + plane :])


def middle_kernel(
    info_ref,
    mixed_ref,
    ffn_own_ref,
    ffn_other_ref,
    back_own_ref,
    back_other_ref,
    gain_ref,
    cot_ref,
    weight_ref,
    *refs,
):
    head_refs = refs[: plane - 1]
    layer_ref, grad_ref, rounded_ref, row_ref = refs[plane - 1 : plane + 3]
    pack_refs = refs[plane + 3 : 2 * plane + 2]
    send_refs = refs[2 * plane + 2 : -1]
    blocks_ref = refs[-1]
    mixed = mixed_ref[...]
    layer_ref[...] = mixed + (ffn_own_ref[...].astype(f32) + ffn_other_ref[...].astype(f32))
    found = back_own_ref[...].astype(f32) + back_other_ref[...].astype(f32)
    stat = lax.rsqrt(jnp.mean(mixed * mixed, axis=1, keepdims=True) + eps_norm)
    row_ref[...] = jnp.broadcast_to(
        jnp.sum(found * mixed * stat, axis=0, keepdims=True), row_ref.shape
    )
    grad = cot_ref[...].astype(f32) + rms_back(found * gain_ref[...], mixed, stat)
    grad_ref[...] = grad
    rounded = grad.astype(bf16)
    rounded_ref[...] = rounded
    attended = dot_f32(rounded, weight_ref[...], 1, 0).astype(bf16)
    for head in range(blocks_ref.shape[0]):
        blocks_ref[head] = attended[:, head * lanes : (head + 1) * lanes]
    for flip, send_ref in enumerate(send_refs):
        send_ref[...] = blocks_ref[info_ref[at_level] ^ flip]
    half, model_width = mixed.shape[0] // 2, mixed.shape[1]
    half_rows = pl.ds(pl.multiple_of(info_ref[at_core] * half, half), half)
    for pack_ref, head_ref in zip(pack_refs, head_refs):
        pack_ref[:, :model_width] = rounded_ref[half_rows, :]
        pack_ref[:, model_width : model_width + lanes] = head_ref[:half, :]
        pack_ref[:, model_width + lanes :] = head_ref[half:, :]


def turn_back_kernel(head_dim, info_ref, *refs):
    count = (len(refs) - 14 - plane) // 2
    block_refs = refs[:count]
    other_refs = refs[count : 2 * count]
    (
        query_ref,
        key_ref,
        q_gain_ref,
        k_gain_ref,
        cos_ref,
        sin_ref,
        query_w_ref,
        key_w_ref,
        value_w_ref,
        part_ref,
        gain_row_ref,
    ) = refs[2 * count : 2 * count + 11]
    send_refs = refs[2 * count + 11 : 2 * count + 11 + plane]
    query_buf, pair_buf, raw_ref = refs[2 * count + 11 + plane :]
    kv_heads = count
    for flip in range(count):
        head = info_ref[at_level] ^ flip
        query_buf[head] = block_refs[flip][...]
        pair_buf[head] = other_refs[flip][...].astype(f32)
    table = head_table(head_dim)
    cosine = cos_ref[...]
    sine = sin_ref[...]
    q_gain_row = jnp.concatenate([q_gain_ref[...]] * (lanes // head_dim), axis=1)
    k_gain_row = jnp.concatenate([k_gain_ref[...]] * (lanes // head_dim), axis=1)
    lane = lax.broadcasted_iota(jnp.int32, cosine.shape, 1)

    def back(grad_rot, raw, gain):
        grad_norm = grad_rot * cosine - swap_halves(grad_rot, head_dim) * sine
        stat = lax.rsqrt(split_dot(raw * raw, table) + eps_norm)
        gain_row = jnp.sum(grad_norm * raw * stat, axis=0, keepdims=True)
        grad_in = grad_norm * gain
        grad_raw = stat * grad_in - raw * stat**3 * split_dot(grad_in * raw, table)
        return (grad_raw.astype(bf16), gain_row)

    total = None
    gain_rows = [None, None]
    place = 0
    per_slot = raw_ref.shape[2] // lanes

    def emit(tile, weight, kind, gain_row):
        nonlocal total, place
        slot = place % per_slot
        raw_ref[place // per_slot, :, slot * lanes : (slot + 1) * lanes] = tile
        place += 1
        found = dot_f32(tile, weight, 1, 1)
        total = found if total is None else total + found
        if gain_row is not None:
            gain_rows[kind] = gain_row if gain_rows[kind] is None else gain_rows[kind] + gain_row

    for head in range(kv_heads):
        cols = slice(head * lanes, (head + 1) * lanes)
        tile, gain_row = back(query_buf[head].astype(f32), query_ref[:, cols], q_gain_row)
        emit(tile, query_w_ref[:, cols], 0, gain_row)
    for pair in range(kv_heads // 2):
        cols = slice(pair * lanes, (pair + 1) * lanes)
        first = pair_buf[2 * pair]
        second = pair_buf[2 * pair + 1]
        merged = jnp.where(lane < head_dim, first, pltpu.roll(second, head_dim, 1))
        tile, gain_row = back(merged, key_ref[:, cols], k_gain_row)
        emit(tile, key_w_ref[:, cols], 1, gain_row)
    for pair in range(kv_heads // 2):
        cols = slice(pair * lanes, (pair + 1) * lanes)
        first = pair_buf[2 * pair]
        second = pair_buf[2 * pair + 1]
        merged = jnp.where(lane < head_dim, pltpu.roll(first, head_dim, 1), second).astype(bf16)
        emit(merged, value_w_ref[:, cols], 1, None)
    part_ref[...] = total.astype(bf16)
    gain_row_ref[...] = jnp.concatenate(gain_rows + [jnp.zeros((6, lanes), f32)], axis=0)
    for flip in range(plane):
        send_refs[flip][...] = raw_ref[info_ref[at_place] ^ flip]


def last_kernel(tokens_ref, grad_ref, own_ref, other_ref, gain_ref, out_ref, row_ref):
    rows = tokens_ref[...].astype(f32)
    stat = lax.rsqrt(jnp.mean(rows * rows, axis=1, keepdims=True) + eps_norm)
    found = own_ref[...].astype(f32) + other_ref[...].astype(f32)
    row_ref[...] = jnp.broadcast_to(
        jnp.sum(found * rows * stat, axis=0, keepdims=True), row_ref.shape
    )
    out_ref[...] = grad_ref[...] + rms_back(found * gain_ref[...], rows, stat)


def plane_gather(mine):
    near = [xor_swap(mine, everywhere, flip) for flip in range(1, plane)]
    far = [xor_swap(found, "tp", 1) for found in near]
    return (near, far)


def window(cols):
    half = cols // 2
    width = min(half, -(-half // (2 * lanes)) * lanes)
    return (half, width)


def rows_kernel(jobs, steps, info_ref, *refs):
    step = pl.program_id(0)
    gain_refs = refs[-5 - 2 * len(jobs) : -2 - 2 * len(jobs)]
    send_ref, keep_ref = refs[-2 - 2 * len(jobs) : -2 * len(jobs)]
    bufs = refs[-2 * len(jobs) :]
    height = keep_ref.shape[1]
    core = info_ref[at_core]
    used = 0
    offset = 0
    pieces = []
    for number, (packed, width) in enumerate(jobs):
        row_buf, col_buf = bufs[2 * number : 2 * number + 2]
        own_ref = refs[used]
        near_refs = refs[used + 1 : used + plane]
        far_refs = refs[used + plane : used + 2 * plane - 1]
        used += 2 * plane - 1
        row_count = own_ref.shape[0]
        half = row_count // 2
        col_count = 2 * plane - 1 if packed else plane
        col_refs = refs[used : used + col_count]
        used += col_count

        @pl.when(step == 0)
        def _():
            if packed:
                col_buf[:row_count, :] = col_refs[0][...]
                for n, col_ref in enumerate(col_refs[1:]):
                    start = row_count + n * half
                    col_buf[start : start + half, :] = col_ref[...]
            else:
                for n, col_ref in enumerate(col_refs):
                    col_buf[n * row_count : (n + 1) * row_count, :] = col_ref[...]

        row_buf[:row_count, :] = own_ref[...]
        for n in range(plane - 1):
            base = (n + 1) * row_count
            near_rows = pl.ds(pl.multiple_of(base + core * half, half), half)
            far_rows = pl.ds(pl.multiple_of(base + (1 - core) * half, half), half)
            row_buf[near_rows, :] = near_refs[n][...]
            row_buf[far_rows, :] = far_refs[n][...]
        pieces.append((offset, width, dot_f32(row_buf[...], col_buf[...], 0, 0)))
        offset += width
    if offset < keep_ref.shape[2]:
        ffn_ref, attn_ref, head_ref = gain_refs
        rows = [ffn_ref[:1, :], attn_ref[:1, :]]
        for n in range(2):
            rows.append(jnp.concatenate([head_ref[n : n + 1, :]] * (height // lanes), axis=1))
        rows.append(jnp.zeros((lanes - 4, height), f32))
        pieces.append((offset, lanes, jnp.concatenate(rows, axis=0).T))

    @pl.when(step < steps)
    def _():
        for offset, width, found in pieces:
            send_ref[0, :, offset : offset + width] = found.astype(bf16)

    @pl.when(step >= steps)
    def _():
        for offset, width, found in pieces:
            keep_ref[0, :, offset : offset + width] = found


def fold_kernel(info_ref, kept_ref, found_ref, send_ref, keep_ref, *, slot):
    bit = info_ref[at_bits + slot]
    send_ref[...] = (kept_ref[1 - bit] + found_ref[1 - bit].astype(f32)).astype(bf16)
    keep_ref[...] = kept_ref[bit] + found_ref[bit].astype(f32)


def finish_kernel(jobs, info_ref, *refs):
    out_refs = refs[2 * jobs :]
    height = out_refs[0].shape[0]
    for flip, out_ref in enumerate(out_refs):
        start = pl.multiple_of((info_ref[at_place] ^ flip) * height, height)
        rows = pl.ds(start, height)
        offset = 0
        for n in range(jobs):
            kept_ref, found_ref = refs[2 * n : 2 * n + 2]
            width = kept_ref.shape[1]
            total = kept_ref[rows, :] + found_ref[rows, :].astype(f32)
            out_ref[:, offset : offset + width] = total.astype(out_ref.dtype)
            offset += width


class Halving:
    def __init__(self, index, total, model_width):
        self.blocks = total // plane
        self.model_width = model_width
        bits = self.blocks.bit_length() - 1
        self.fine = self.blocks == 4 and model_width // self.blocks % lanes == 0
        self.order = list(range(bits)) if self.fine else list(range(bits))[::-1]
        self.steps = 2 if self.fine else 1
        self.height = model_width // self.steps // 2
        block_index = index // plane
        self.bits = [(block_index >> bit) & 1 for bit in self.order]

    def rows(self, info, jobs, gains=None):
        steps, height = self.steps, self.height
        per_piece = self.model_width // height

        def block_of(step, info_ref):
            first = info_ref[at_bits]
            bit = jnp.where(step < steps, 1 - first, first)
            return 2 * (step % steps) + bit if steps > 1 else bit

        fixed = lambda *shape: pl.BlockSpec(shape, lambda step, info_ref: (0,) * len(shape))
        args, specs, scratch, shape_jobs = [], [], [], []
        flops = 0
        for (own, near, far, slot), cols in jobs:
            row_count = own.shape[0]
            half = row_count // 2
            packed = len(cols) == 1
            width = cols[0].shape[1]
            args += [own, *near, *far]
            specs.append(
                pl.BlockSpec((row_count, height), lambda step, ref: (0, block_of(step, ref)))
            )
            specs += [
                pl.BlockSpec(
                    (half, height),
                    lambda step, ref, base=slot * per_piece: (0, base + block_of(step, ref)),
                )
            ] * (2 * plane - 2)
            args.append(cols[0])
            specs.append(fixed(row_count, width))
            if packed:
                for part in near:
                    for n in range(2):
                        args.append(part)
                        spot = self.model_width // width + n
                        specs.append(
                            pl.BlockSpec((half, width), lambda step, ref, spot=spot: (0, spot))
                        )
            else:
                args += cols[1:]
                specs += [fixed(row_count, width)] * (plane - 1)
            scratch += [
                pltpu.VMEM((plane * row_count, height), bf16),
                pltpu.VMEM((plane * row_count, width), bf16),
            ]
            shape_jobs.append((packed, width))
            flops += 2 * plane * row_count * self.model_width * width
        total_width = sum(width for _, width in shape_jobs)
        if gains is not None:
            total_width += lanes
            row_spec = pl.BlockSpec((8, height), lambda step, ref: (0, block_of(step, ref)))
            specs += [row_spec, row_spec, fixed(8, lanes)]
        else:
            gains = [jnp.zeros((8, lanes), f32)] * 3
            specs += [fixed(8, lanes)] * 3
        args += gains
        out = (1, height, total_width)
        return pl.pallas_call(
            functools.partial(rows_kernel, shape_jobs, steps),
            grid_spec=pltpu.PrefetchScalarGridSpec(
                num_scalar_prefetch=1,
                grid=(2 * steps,),
                in_specs=specs,
                out_specs=[
                    pl.BlockSpec(out, lambda step, ref: (jnp.minimum(step, steps - 1), 0, 0)),
                    pl.BlockSpec(out, lambda step, ref: (jnp.maximum(step - steps, 0), 0, 0)),
                ],
                scratch_shapes=scratch,
            ),
            out_shape=[
                shape_of((steps, height, total_width), bf16),
                shape_of((steps, height, total_width), f32),
            ],
            cost_estimate=pl.CostEstimate(
                flops=flops,
                bytes_accessed=sum(arg.size * arg.dtype.itemsize for arg in args)
                + 6 * steps * height * total_width,
                transcendentals=0,
            ),
            compiler_params=pltpu.CompilerParams(vmem_limit_bytes=vmem_limit),
            name="rows",
        )(info, *args)

    def start(self, turn, sent):
        return xor_swap(sent, everywhere, plane << self.order[turn])

    def fold(self, info, turn, kept, found):
        width = kept.shape[-1]
        rows_left = kept.size // width // 2
        send, keep = whole_call(
            functools.partial(fold_kernel, slot=turn),
            [shape_of((rows_left, width), bf16), shape_of((rows_left, width), f32)],
            [kept.reshape(2, rows_left, width), found.reshape(2, rows_left, width)],
            scalars=(info,),
        )
        return (keep, self.start(turn, send))

    def through(self, info, rows):
        sent, kept = rows
        found = self.start(0, sent)
        for turn in range(1, len(self.order)):
            kept, found = self.fold(info, turn, kept, found)
        return (kept.reshape(-1, kept.shape[-1]), found.reshape(-1, kept.shape[-1]))


def return_rows(info, sums):
    height = sums[0][0].shape[0] // plane
    width = sum(kept.shape[1] for kept, _ in sums)
    parts = whole_call(
        functools.partial(finish_kernel, len(sums)),
        [shape_of((height, width), bf16 if flip else f32) for flip in range(plane)],
        [value for pair in sums for value in pair],
        scalars=(info,),
    )
    return plane_swap(parts)


def assemble_kernel(moves, gain_start, info_ref, *refs):
    part_refs = refs[:plane]
    out_refs = refs[plane:]
    for flip in range(plane):
        for member in range(plane):

            @pl.when((info_ref[at_place] ^ flip) == member)
            def _():
                for out, out_start, start, width in moves[member]:
                    out_refs[out][:, out_start : out_start + width] = part_refs[flip][
                        :, start : start + width
                    ].astype(f32)

    if gain_start is not None:
        cols = slice(gain_start, gain_start + lanes)
        total = sum(part_ref[:, cols].astype(f32) for part_ref in part_refs).T
        for n in range(4):
            out_refs[len(out_refs) - 4 + n][...] = total[n : n + 1, :]


def assemble(info, parts, moves, widths, gain_start=None):
    height = parts[0].shape[0]
    outs = [shape_of((height, width), f32) for width in widths]
    if gain_start is not None:
        outs += [shape_of((1, height), f32)] * 4
    return whole_call(
        functools.partial(assemble_kernel, moves, gain_start), outs, parts, scalars=(info,)
    )


def shards(
    tokens,
    positions,
    attn_gain,
    ffn_gain,
    q_gain,
    k_gain,
    w_query,
    w_key,
    w_value,
    w_out,
    w_gate,
    w_up,
    w_down,
    cotangent,
):
    seq_count, block_len, model_width = tokens.shape
    row_count = seq_count * block_len
    head_dim = q_gain.shape[0]
    q_heads = w_query.shape[1] // head_dim
    kv_heads = w_key.shape[1] // head_dim
    key_width = kv_heads * head_dim
    query_width = q_heads * head_dim
    group_size = q_heads // kv_heads
    hidden_width = w_gate.shape[1]
    ctx_size = lax.axis_size("ctx")
    total = ctx_size * lax.axis_size("seq")
    here_index = lax.axis_index("ctx")
    index = lax.axis_index(everywhere)
    by_head = ctx_size == 2 * kv_heads
    rows_bf = shape_of((row_count, model_width), bf16)
    rows_f32 = shape_of((row_count, model_width), f32)
    head_block = shape_of((row_count, lanes), bf16)
    full_block = shape_of((row_count + pos_rows, lanes), bf16)
    halving = Halving(index, total, model_width)
    info = jnp.stack(
        [
            here_index // 2 if by_head else jnp.int32(0),
            here_index % 2,
            lax.axis_index("tp"),
            index % plane,
            *halving.bits,
        ]
    ).astype(jnp.int32)

    cot_rows = cotangent.reshape(row_count, model_width)
    token_rows = tokens.reshape(row_count, model_width)
    pack_width = 2 * lanes
    q_gain_row = q_gain[None, :]
    k_gain_row = k_gain[None, :]
    attn_gain_row = attn_gain[None, :]
    ffn_gain_row = ffn_gain[None, :]

    normed_one, early_half, query_raw, key_raw, cosine, sine, *found = whole_call(
        functools.partial(front_kernel, head_dim),
        [
            rows_bf,
            shape_of((row_count // 2, 2 * model_width), bf16),
            shape_of((row_count, query_width), f32),
            shape_of((row_count, key_width), f32),
            shape_of((row_count, lanes), f32),
            shape_of((row_count, lanes), f32),
        ]
        + [full_block] * kv_heads
        + [head_block] * kv_heads,
        [
            token_rows,
            cot_rows,
            attn_gain_row,
            w_query,
            w_key,
            w_value,
            q_gain_row,
            k_gain_row,
            positions,
        ],
        scalars=(info,),
        scratch=[
            pltpu.VMEM((kv_heads, row_count + pos_rows, lanes), bf16),
            pltpu.VMEM((kv_heads, row_count, lanes), bf16),
        ],
        flops=2 * row_count * model_width * (query_width + 2 * key_width),
    )
    packed, pair_parts = found[:kv_heads], found[kv_heads:]

    if by_head:
        pairs = level_swap(pair_parts)
        blocks = level_swap(packed)
        sources = [*blocks, *pairs, *side_swap(pairs)]
        out_heads, log_sum, out_parts = head_forward(info, sources, seq_count, head_dim)
        out_blocks = level_swap(out_parts)
    else:
        flat = jnp.concatenate(
            [jnp.stack([part[:row_count] for part in packed]), jnp.stack(pair_parts)], axis=2
        )
        flat = flat.reshape(kv_heads, seq_count, block_len, pack_width)
        flat = jnp.transpose(flat, (1, 2, 0, 3))
        query_grouped = flat[..., :lanes].reshape(
            seq_count, block_len, kv_heads, group_size, head_dim
        )
        query_index = here_index * block_len + jnp.arange(block_len, dtype=jnp.int32)
        lowest_key = query_index[None, :] - positions
        attended_grouped, log_sum, key_all, value_all = gathered_forward(
            query_grouped,
            flat[..., lanes : lanes + head_dim].reshape(seq_count, block_len, key_width),
            flat[..., lanes + head_dim :].reshape(seq_count, block_len, key_width),
            query_index,
            lowest_key,
        )
        out_blocks = list(
            jnp.transpose(attended_grouped, (2, 0, 1, 3, 4)).reshape(kv_heads, row_count, lanes)
        )

    early_near, early_far = plane_gather(early_half)
    cot_pieces = (cot_rows, early_near, early_far, 0)
    one_pieces = (normed_one, early_near, early_far, 1)

    attn_part, *head_parts = whole_call(
        project_kernel,
        [rows_bf] + [head_block] * plane,
        [*out_blocks, w_out],
        scalars=(info,),
        scratch=[pltpu.VMEM((kv_heads, row_count, lanes), bf16)],
        flops=2 * row_count * model_width * query_width,
    )
    mixed, normed_two, two_half, ffn_part, back_part, hidden_parts, both_parts = ffn_call(
        info,
        token_rows,
        attn_part,
        named_swap(attn_part),
        ffn_gain_row,
        cot_rows,
        w_gate,
        w_up,
        w_down,
    )
    ffn_other = named_swap(ffn_part)
    back_other = named_swap(back_part)
    hidden_plane = plane_swap(hidden_parts)
    both_plane = plane_swap(both_parts)
    two_near, two_far = plane_gather(two_half)
    two_pieces = (normed_two, two_near, two_far, 0)
    half, width = window(hidden_width)

    pack_block = shape_of((row_count // 2, model_width + 2 * lanes), bf16)
    layer_output, grad_mixed, grad_mixed_bf, ffn_row, *found = whole_call(
        middle_kernel,
        [rows_f32, rows_f32, rows_bf, shape_of((8, model_width), f32)]
        + [pack_block] * (plane - 1)
        + [head_block] * kv_heads,
        [
            mixed,
            ffn_part,
            ffn_other,
            back_part,
            back_other,
            ffn_gain_row,
            cot_rows,
            w_out,
            *head_parts[1:],
        ],
        scalars=(info,),
        scratch=[pltpu.VMEM((kv_heads, row_count, lanes), bf16)],
        flops=2 * row_count * model_width * query_width,
    )
    mixed_packs, grad_parts = found[: plane - 1], found[plane - 1 :]

    if by_head:
        grads = level_swap(grad_parts)
        query_parts, own_parts, other_parts = head_backward(
            info, sources, grads, out_heads, log_sum, seq_count, head_dim
        )
        crossed = side_swap(other_parts)
        returned = level_swap(query_parts)
        pair_sums = whole_call(
            functools.partial(merge_kernel, kv_heads),
            [head_block] * kv_heads,
            [*own_parts, *crossed],
        )
        others = level_swap(pair_sums)
    else:
        grad_grouped = jnp.transpose(
            jnp.stack(grad_parts).reshape(kv_heads, seq_count, block_len, group_size, head_dim),
            (1, 2, 0, 3, 4),
        )
        query_grad, key_grad_own, value_grad_own = gathered_backward(
            query_grouped,
            grad_grouped,
            attended_grouped,
            log_sum,
            key_all,
            value_all,
            query_index,
            lowest_key,
        )
        shaped = lambda grad: grad.reshape(seq_count, block_len, kv_heads, -1)
        returned = jnp.concatenate(
            [shaped(query_grad), shaped(key_grad_own), shaped(value_grad_own)], axis=-1
        ).astype(bf16)
        returned = jnp.transpose(returned, (2, 0, 1, 3)).reshape(kv_heads, row_count, pack_width)
        others = list(returned[..., lanes:])
        returned = list(returned[..., :lanes])

    down_sum = halving.through(info, halving.rows(info, [(cot_pieces, hidden_plane)]))
    both_sum = halving.through(info, halving.rows(info, [(two_pieces, both_plane)]))
    wide_parts = return_rows(info, [both_sum, down_sum])

    mixed_near = [xor_swap(pack, everywhere, flip + 1) for flip, pack in enumerate(mixed_packs)]
    mixed_far = [xor_swap(found, "tp", 1) for found in mixed_near]
    mixed_pieces = (grad_mixed_bf, mixed_near, mixed_far, 0)

    raw_width = (query_width + 2 * key_width) // plane
    one_part, head_rows, *raw_parts = whole_call(
        functools.partial(turn_back_kernel, head_dim),
        [rows_bf, shape_of((8, lanes), f32)] + [shape_of((row_count, raw_width), bf16)] * plane,
        [
            *returned,
            *others,
            query_raw,
            key_raw,
            q_gain_row,
            k_gain_row,
            cosine,
            sine,
            w_query,
            w_key,
            w_value,
        ],
        scalars=(info,),
        scratch=[
            pltpu.VMEM((kv_heads, row_count, lanes), bf16),
            pltpu.VMEM((kv_heads, row_count, lanes), f32),
            pltpu.VMEM((plane, row_count, raw_width), bf16),
        ],
        flops=2 * row_count * model_width * (query_width + 2 * key_width),
    )
    one_other = named_swap(one_part)
    head_sum = head_rows + named_swap(head_rows)
    head_sum = head_sum + jnp.roll(head_sum, head_dim, axis=1)
    raw_plane = plane_swap(raw_parts)
    input_grad, attn_row = whole_call(
        last_kernel,
        [rows_f32, shape_of((8, model_width), f32)],
        [token_rows, grad_mixed, one_part, one_other, attn_gain_row],
    )

    late_sum = halving.through(
        info,
        halving.rows(
            info,
            [(mixed_pieces, head_parts[:1]), (one_pieces, raw_plane)],
            [ffn_row, attn_row, head_sum],
        ),
    )
    late_parts = return_rows(info, [late_sum])

    skip = 2 * width - half
    wide_moves = []
    for member in range(plane):
        far_side = member // 2
        down_start = half * (member % 2) + far_side * width
        wide_moves.append(
            [
                (member % 2, half * far_side, 0, half),
                (2, down_start, half + far_side * skip, width - far_side * skip),
            ]
        )
    wgate_grad, wup_grad, wdown_grad = assemble(info, wide_parts, wide_moves, [hidden_width] * 3)

    out_width = lanes
    late_moves = []
    for member in range(plane):
        moves = [(0, member * out_width, 0, out_width)]
        for out, begin, size in (
            (1, 0, query_width),
            (2, query_width, key_width),
            (3, query_width + key_width, key_width),
        ):
            low = max(begin, member * raw_width)
            high = min(begin + size, (member + 1) * raw_width)
            if low < high:
                moves.append((out, low - begin, out_width + low - member * raw_width, high - low))
        late_moves.append(moves)
    wo_grad, wq_grad, wk_grad, wv_grad, *gain_rows = assemble(
        info,
        late_parts,
        late_moves,
        [query_width, query_width, key_width, key_width],
        out_width + raw_width,
    )
    ffngain_grad, attngain_grad, qgain_grad, kgain_grad = (row.reshape(-1) for row in gain_rows)
    if qgain_grad.shape[0] < head_dim:
        qgain_grad, kgain_grad = (
            lax.all_gather(row, everywhere, axis=0, tiled=True)[:head_dim]
            for row in (qgain_grad, kgain_grad)
        )
    else:
        qgain_grad, kgain_grad = qgain_grad[:head_dim], kgain_grad[:head_dim]
    return (
        layer_output.reshape(seq_count, block_len, model_width),
        input_grad.reshape(seq_count, block_len, model_width),
        wq_grad,
        wk_grad,
        wv_grad,
        wo_grad,
        wgate_grad,
        wup_grad,
        wdown_grad,
        attngain_grad,
        ffngain_grad,
        qgain_grad,
        kgain_grad,
    )


def solution(mesh):
    placed = (
        P("seq", "ctx", None),
        P("seq", "ctx"),
        P(),
        P(),
        P(),
        P(),
        P(None, "tp"),
        P(None, "tp"),
        P(None, "tp"),
        P(None, "tp"),
        P(None, "tp"),
        P(None, "tp"),
        P(None, "tp"),
        P("seq", "ctx", None),
    )
    return jax.shard_map(
        shards,
        mesh=mesh,
        in_specs=placed,
        out_specs=(
            P("seq", "ctx", None),
            P("seq", "ctx", None),
            P(("ctx", "seq"), "tp"),
            P(("ctx", "seq"), "tp"),
            P(("ctx", "seq"), "tp"),
            P(("ctx", "seq"), "tp"),
            P(("ctx", "seq"), "tp"),
            P(("ctx", "seq"), "tp"),
            P(("ctx", "seq"), "tp"),
            P(("ctx", "seq")),
            P(("ctx", "seq")),
            P(),
            P(),
        ),
        check_vma=False,
    )
```

time: 294 us -> 273 us (0.929)
  Pallas kernels: 89 us -> 57.1 us
  waiting for transfers between devices: 96.8 us -> 128 us
  local copies, waits for them, and re-layouts: 24.7 us -> 12.9 us
  other arithmetic: 6.66 us -> 0.08 us
    ppermute x64 -> x70, waiting for transfers between devices: 96.8 us -> 128 us  [xor_swap(): lax.ppermute(value, axis, [(index, index ^ flip) for index in range(size)])]
    pallas_call x9 -> x4, Pallas kernels: 47.7 us -> 27.9 us  [the longest x3 15.2 us: rows(): pl.pallas_call(functools.partial(rows_kernel, shape_jobs, steps), grid_sp...]
    squeeze x9 -> x0, local copies, waits for them, and re-layouts: 12.8 us -> none  [pick(): return lax.dynamic_index_in_dim(value, index, axis, keepdims=False)]
    pallas_call x10 -> x15, Pallas kernels: 41.3 us -> 29.2 us  [whole_call(): pl.pallas_call(kernel, out_shape=tuple(outs), in_specs=[smem_spec()] * le...]
    unnamed x124 -> x44, local copies, waits for them, and re-layouts: 4.43 us -> 12.8 us
    slice x9 -> x1, local copies, waits for them, and re-layouts: 3.68 us -> 0.07 us  [shards(): head_sum = head_sum + jnp.roll(head_sum, head_dim, axis=1)]
    add x8 -> x2, other arithmetic: 3.3 us -> 0.08 us  [the longest x1 0.08 us: shards(): head_sum = head_sum + jnp.roll(head_sum, head_dim, axis=1)]
    dynamic_slice x5 -> x0, local copies, waits for them, and re-layouts: 3.19 us -> none  [the longest x1 2.41 us: take_hidden(): return lax.dynamic_slice_in_dim(hidden, start, width, 1)]
  transfers between devices with their start and end apart: 64 -> 70, of which waited for: 17 -> 27; matrix products, arithmetic and copies ran while one was open for 8% -> 0% of each run, Pallas kernels for 26% -> 18%
where the time goes in v1:
time: 273 us; the launch traced here: 272 us
  waiting for transfers between devices  128 us (47%)
  starting transfers between devices  72.9 us (27%)
  Pallas kernels  57.1 us (21%)
  local copies, waits for them, and re-layouts  12.9 us (5%)
    ppermute x70, waiting for transfers between devices, xor_swap(): lax.ppermute(value, axis, [(index, index ^ flip) for index in range(size)])  128 us
    ppermute x70, starting transfers between devices, xor_swap(): lax.ppermute(value, axis, [(index, index ^ flip) for index in range(size)])  72.9 us
    pallas_call x15, Pallas kernels, whole_call(): pl.pallas_call(kernel, out_shape=tuple(outs), in_specs=[smem_spec()] * le...  29.2 us
    pallas_call x3, Pallas kernels, rows(): pl.pallas_call(functools.partial(rows_kernel, shape_jobs, steps), grid_sp...  15.2 us
    unnamed x44, local copies, waits for them, and re-layouts  12.8 us
    pallas_call x1, Pallas kernels, ffn_call(): pl.pallas_call(functools.partial(ffn_kernel, steps), grid_spec=pltpu.Pref...  12.7 us
  transfers between devices with their start and end apart: 70, of which 27 were waited for; matrix products, arithmetic and copies ran while one was open for 0% of the time, Pallas kernels for 18%

profile of v1, /device:TPU:0, one launch (start us, length us, event | category | flops | bytes accessed | tf_op | source)
XLA Modules:
  0.0 272.4 jit_solution(8842191753156080048)
XLA Ops:
  11.4 3.1 %collective-permute-start.3 = (bf16[256,128]{1,0:T(8,128)(2,1)S(1)}, bf16[256,128]{1,0:T(8,128)(2,1)S(1)}, u32[]{:S(2)}, u32[]{:S(2)}) collective-permute-start(bf16[256,128]{1,0:T(8,128)(2,1)S(1)} %get-tuple-element.122), channel_id=1, source_target_pairs={{0,8},{4,12},{8,0},{12,4},{16,24},{20,28},{24,16},{28,20},{1,9},{5... | collective-permute-start | bytes 196616 | tf_op jit(solution)/shard_map/ppermute | solution.py:39
  14.5 2.6 collective-permute-start.4
  31.6 4.8 %shard_map.238 = (bf16[4,256,128]{2,1,0:T(8,128)(2,1)S(1)}, f32[8,256]{1,0:T(8,128)S(1)}, bf16[256,128]{1,0:T(8,128)(2,1)S(1)}, bf16[256,128]{1,0:T(8,128)(2,1)S...) custom-call(s32[6]{0:T(128)S(1)} %stack.27.info_ref.refs_0_, ...), custom_call_target="tpu_custom_call" | custom-call | flops 1073741824 | bytes 1335296 | tf_op jit(solution)/shard_map/pallas_call | solution.py:242
  55.1 12.7 %ffn.1 = (f32[256,1024]{1,0:T(8,128)S(1)}, bf16[256,1024]{1,0:T(8,128)(2,1)S(1)}, bf16[128,1024]{1,0:T(8,128)(2,1)S(1)}, bf16[256,1024]{1,0:T(8,128)(2,1)S(1)}, ...) custom-call(s32[6]{0:T(128)S(1)} %stack.27.info_ref.refs_0_, ...), custom_call_target="tpu_custom_call" | custom-call | flops 9663676416 | bytes 14155776 | tf_op jit(solution)/shard_map/ffn/pallas_call | solution.py:585
  71.3 2.7 collective-permute-done.38.refs_17_.refs_3_
  74.0 5.5 %collective-permute-done.51.refs_1_ = bf16[128,1024]{1,0:T(8,128)(2,1)S(1)} collective-permute-done((bf16[128,1024]{1,0:T(8,128)(2,1)S(1)}, bf16[128,1024]{1,0:T(8,128)(2,1)S(1)}, u32[]{:S(2)}, u32[]{:S(2)}) %collective-permute-start.51) | collective-permute-done | bytes 262176 | tf_op jit(solution)/shard_map/ppermute | solution.py:39
  80.1 4.7 %collective-permute-done.53.refs_3_ = bf16[128,1024]{1,0:T(8,128)(2,1)S(1)} collective-permute-done((bf16[128,1024]{1,0:T(8,128)(2,1)S(1)}, bf16[128,1024]{1,0:T(8,128)(2,1)S(1)}, u32[]{:S(2)}, u32[]{:S(2)}) %collective-permute-start.53) | collective-permute-done | bytes 262176 | tf_op jit(solution)/shard_map/ppermute | solution.py:39
  86.5 8.3 %collective-permute-done.62.refs_8_ = bf16[256,640]{1,0:T(8,128)(2,1)S(1)} collective-permute-done((bf16[256,640]{1,0:T(8,128)(2,1)S(1)}, bf16[256,640]{1,0:T(8,128)(2,1)S(1)}, u32[]{:S(2)}, u32[]{:S(2)}) %collective-permute-start.62) | collective-permute-done | bytes 327712 | tf_op jit(solution)/shard_map/ppermute | solution.py:39
  98.4 2.8 %shard_map.240 = (f32[256,1024]{1,0:T(8,128)}, f32[256,1024]{1,0:T(8,128)S(1)}, bf16[256,1024]{1,0:T(8,128)(2,1)S(1)}, f32[8,1024]{1,0:T(8,128)S(1)}, bf16[128,1...) custom-call(s32[6]{0:T(128)S(1)} %stack.27.info_ref.refs_0_, ...), custom_call_target="tpu_custom_call" | custom-call | flops 268435456 | bytes 8818688 | tf_op jit(solution)/shard_map/pallas_call | solution.py:242
  109.0 2.5 collective-permute-done.18.refs_16_
  111.5 6.4 %shard_map.241 = (bf16[256,128]{1,0:T(8,128)(2,1)S(1)}, bf16[256,128]{1,0:T(8,128)(2,1)S(1)}, bf16[256,128]{1,0:T(8,128)(2,1)S(1)}, bf16[256,128]{1,0:T(8,128)(2...) custom-call(s32[6]{0:T(128)S(1)} %stack.27.info_ref.refs_0_, ...), custom_call_target="tpu_custom_call" | custom-call | flops 2684354560 | bytes 2383872 | tf_op jit(solution)/shard_map/pallas_call | solution.py:242
  121.9 3.3 %collective-permute-done.59.refs_10_ = bf16[256,1152]{1,0:T(8,128)(2,1)S(1)} collective-permute-done((bf16[256,1152]{1,0:T(8,128)(2,1)S(1)}, bf16[256,1152]{1,0:T(8,128)(2,1)S(1)}, u32[]{:S(2)}, u32[]{:S(2)}) %collective-permute-start.59) | collective-permute-done | bytes 589856 | tf_op jit(solution)/shard_map/ppermute | solution.py:39
  130.9 5.6 %rows.4 = (bf16[2,256,1152]{2,1,0:T(8,128)(2,1)S(1)}, f32[2,256,1152]{2,1,0:T(8,128)S(1)}) custom-call(s32[6]{0:T(128)S(1)} %stack.27.info_ref.refs_0_, bf16[256,1024]{1,0:T(8,128)(2,1)S(1)} %get-tuple-element.192.refs_0_, bf16[128,1024]{1,0:T(8,128)(2,1)S(1)} %collective-permute-done.51.refs_1_, bf16[128,1024]{1,0:T(8,128)(2,1)S(1)} %collective-permute-done.52.refs_2_, ...), custom_call_target="tpu_custom_call" | custom-call | flops 2415919104 | bytes 8007680 | tf_op jit(solution)/shard_map/rows/pallas_call | solution.py:909
  141.2 23.9 %collective-permute-done.26.refs_5_ = bf16[256,128]{1,0:T(8,128)(2,1)S(1)} collective-permute-done((bf16[256,128]{1,0:T(8,128)(2,1)S(1)}, bf16[256,128]{1,0:T(8,128)(2,1)S(1)}, u32[]{:S(2)}, u32[]{:S(2)}) %collective-permute-start.26) | collective-permute-done | bytes 65568 | tf_op jit(solution)/shard_map/ppermute | solution.py:39
  168.7 3.0 %shard_map.243 = (bf16[256,1024]{1,0:T(8,128)(2,1)S(1)}, f32[8,128]{1,0:T(8,128)S(1)}, bf16[256,256]{1,0:T(8,128)(2,1)S(1)}, bf16[256,256]{1,0:T(8,128)(2,1)S(1)...) custom-call(s32[6]{0:T(128)S(1)} %stack.27.info_ref.refs_0_, ...), custom_call_target="tpu_custom_call" | custom-call | flops 536870912 | bytes 4723200 | tf_op jit(solution)/shard_map/pallas_call | solution.py:242
  173.1 2.6 collective-permute-done.30.refs_1_.refs_8_.refs_9_
  178.6 3.5 %collective-permute-done.32.refs_3_.refs_12_.refs_13_ = bf16[128,1280]{1,0:T(8,128)(2,1)S(1)} collective-permute-done((bf16[128,1280]{1,0:T(8,128)(2,1)S(1)}, bf16[128,1280]{1,0:T(8,128)(2,1)S(1)}, u32[]{:S(2)}, u32[]{:S(2)}) %collective-permute-start.32) | collective-permute-done | bytes 327712 | tf_op jit(solution)/shard_map/ppermute | solution.py:39
  182.1 2.8 %collective-permute-start.44 = (bf16[256,256]{1,0:T(8,128)(2,1)S(1)}, bf16[256,256]{1,0:T(8,128)(2,1)S(1)}, u32[]{:S(2)}, u32[]{:S(2)}) collective-permute-start(bf16[256,256]{1,0:T(8,128)(2,1)S(1)} %get-tuple-element.176), channel_id=1, source_target_pairs={{0,6},{2,4},{4,2},{6,0},{8,14},{10,12},{12,10},{14,8},{16,22},{18,... | collective-permute-start | bytes 393224 | tf_op jit(solution)/shard_map/ppermute | solution.py:39
  184.9 4.1 %rows.5 = (bf16[2,256,640]{2,1,0:T(8,128)(2,1)S(1)}, f32[2,256,640]{2,1,0:T(8,128)S(1)}) custom-call(s32[6]{0:T(128)S(1)} %stack.27.info_ref.refs_0_, bf16[256,1024]{1,0:T(8,128)(2,1)S(1)} %bitcast.21, bf16[128,2048]{1,0:T(8,128)(2,1)S(1)} %collective-permute-done.36.refs_15_.refs_1_, bf16[128,2048]{1,0:T(8,128)(2,1)S(1)} %collective-permute-done.37.refs_16_.refs_2_, ...), custom_call_target="tpu_custom_call" | custom-call | flops 1342177280 | bytes 6959104 | tf_op jit(solution)/shard_map/rows/pallas_call | solution.py:909
  191.7 5.6 %rows.3 = (bf16[2,256,512]{2,1,0:T(8,128)(2,1)S(1)}, f32[2,256,512]{2,1,0:T(8,128)S(1)}) custom-call(s32[6]{0:T(128)S(1)} %stack.27.info_ref.refs_0_, bf16[256,1024]{1,0:T(8,128)(2,1)S(1)} %get-tuple-element.166.refs_0_, bf16[128,1280]{1,0:T(8,128)(2,1)S(1)} %collective-permute-done.30.refs_1_.refs_8_.refs_9_, ...), custom_call_target="tpu_custom_call" | custom-call | flops 805306368 | bytes 10358784 | tf_op jit(solution)/shard_map/rows/pallas_call | solution.py:909
  200.0 20.0 %collective-permute-done.65.found_ref = bf16[2,256,640]{2,1,0:T(8,128)(2,1)S(1)} collective-permute-done((bf16[2,256,640]{2,1,0:T(8,128)(2,1)S(1)}, bf16[2,256,640]{2,1,0:T(8,128)(2,1)S(1)}, u32[]{:S(2)}, u32[]{:S(2)}) %collective-permute-start.65) | collective-permute-done | bytes 655392 | tf_op jit(solution)/shard_map/ppermute | solution.py:39
  220.8 10.1 %collective-permute-done.46.found_ref = bf16[2,256,512]{2,1,0:T(8,128)(2,1)S(1)} collective-permute-done((bf16[2,256,512]{2,1,0:T(8,128)(2,1)S(1)}, bf16[2,256,512]{2,1,0:T(8,128)(2,1)S(1)}, u32[]{:S(2)}, u32[]{:S(2)}) %collective-permute-start.46) | collective-permute-done | bytes 524320 | tf_op jit(solution)/shard_map/ppermute | solution.py:39
  231.6 18.4 %collective-permute-done.66.refs_3_ = bf16[256,640]{1,0:T(8,128)(2,1)S(1)} collective-permute-done((bf16[256,640]{1,0:T(8,128)(2,1)S(1)}, bf16[256,640]{1,0:T(8,128)(2,1)S(1)}, u32[]{:S(2)}, u32[]{:S(2)}) %collective-permute-start.66) | collective-permute-done | bytes 327712 | tf_op jit(solution)/shard_map/ppermute | solution.py:39
  258.2 5.6 %collective-permute-done.48.refs_1_ = bf16[64,512]{1,0:T(8,128)(2,1)S(1)} collective-permute-done((bf16[64,512]{1,0:T(8,128)(2,1)S(1)}, bf16[64,512]{1,0:T(8,128)(2,1)S(1)}, u32[]{:S(2)}, u32[]{:S(2)}) %collective-permute-start.48) | collective-permute-done | bytes 65568 | tf_op jit(solution)/shard_map/ppermute | solution.py:39
  (184 shorter events, 106.7 us)
Async XLA Ops:
  46.9 23.5 %collective-permute-start.37 = (bf16[128,2048]{1,0:T(8,128)(2,1)S(1)}, bf16[128,2048]{1,0:T(8,128)(2,1)S(1)}, u32[]{:S(2)}, u32[]{:S(2)}) collective-permute-start(bf16[128,2048]{1,0:T(8,128)(2,1)S(1)} %get-tuple-element.172), channel_id=1, source_target_pairs={{0,4},{2,6},{4,0},{6,2},{8,12},{10,14},{12,8},{14,10},{16,20},{18,... | collective-permute-start | bytes 1572872 | tf_op jit(solution)/shard_map/ppermute | solution.py:39
  48.3 25.7 %collective-permute-start.38 = (bf16[128,2048]{1,0:T(8,128)(2,1)S(1)}, bf16[128,2048]{1,0:T(8,128)(2,1)S(1)}, u32[]{:S(2)}, u32[]{:S(2)}) collective-permute-start(bf16[128,2048]{1,0:T(8,128)(2,1)S(1)} %get-tuple-element.172), channel_id=1, source_target_pairs={{0,6},{2,4},{4,2},{6,0},{8,14},{10,12},{12,10},{14,8},{16,22},{18,... | collective-permute-start | bytes 1572872 | tf_op jit(solution)/shard_map/ppermute | solution.py:39
  50.3 34.4 %collective-permute-start.39 = (bf16[128,2048]{1,0:T(8,128)(2,1)S(1)}, bf16[128,2048]{1,0:T(8,128)(2,1)S(1)}, u32[]{:S(2)}, u32[]{:S(2)}) collective-permute-start(bf16[128,2048]{1,0:T(8,128)(2,1)S(1)} %collective-permute-done.36.refs_15_.refs_1_), channel_id=1, source_target_pairs={{0,1},{1,0},{2,3},{3,2},{4,5},{5,4},{6,7},{7,6},{8,9},{9,8},{10,11... | collective-permute-start | bytes 1572872 | tf_op jit(solution)/shard_map/ppermute | solution.py:39
  70.4 14.3 %collective-permute-start.53 = (bf16[128,1024]{1,0:T(8,128)(2,1)S(1)}, bf16[128,1024]{1,0:T(8,128)(2,1)S(1)}, u32[]{:S(2)}, u32[]{:S(2)}) collective-permute-start(bf16[128,1024]{1,0:T(8,128)(2,1)S(1)} %get-tuple-element.193), channel_id=1, source_target_pairs={{0,6},{2,4},{4,2},{6,0},{8,14},{10,12},{12,10},{14,8},{16,22},{18,... | collective-permute-start | bytes 786440 | tf_op jit(solution)/shard_map/ppermute | solution.py:39
  79.6 15.7 %collective-permute-start.14 = (bf16[256,1024]{1,0:T(8,128)(2,1)S(1)}, bf16[256,1024]{1,0:T(8,128)(2,1)S(1)}, u32[]{:S(2)}, u32[]{:S(2)}) collective-permute-start(bf16[256,1024]{1,0:T(8,128)(2,1)S(1)} %get-tuple-element.131.ffn_own_ref), channel_id=1, source_target_pairs={{0,1},{1,0},{2,3},{3,2},{4,5},{5,4},{6,7},{7,6},{8,9},{9,8},{10,11... | collective-permute-start | bytes 1572872 | tf_op jit(solution)/shard_map/ppermute | solution.py:39
  85.2 16.0 %collective-permute-start.63 = (bf16[256,640]{1,0:T(8,128)(2,1)S(1)}, bf16[256,640]{1,0:T(8,128)(2,1)S(1)}, u32[]{:S(2)}, u32[]{:S(2)}) collective-permute-start(bf16[256,640]{1,0:T(8,128)(2,1)S(1)} %get-tuple-element.204), channel_id=1, source_target_pairs={{0,4},{2,6},{4,0},{6,2},{8,12},{10,14},{12,8},{14,10},{16,20},{18,... | collective-permute-start | bytes 983048 | tf_op jit(solution)/shard_map/ppermute | solution.py:39
  86.5 15.4 %collective-permute-start.54 = (bf16[128,1024]{1,0:T(8,128)(2,1)S(1)}, bf16[128,1024]{1,0:T(8,128)(2,1)S(1)}, u32[]{:S(2)}, u32[]{:S(2)}) collective-permute-start(bf16[128,1024]{1,0:T(8,128)(2,1)S(1)} %collective-permute-done.51.refs_1_), channel_id=1, source_target_pairs={{0,1},{1,0},{2,3},{3,2},{4,5},{5,4},{6,7},{7,6},{8,9},{9,8},{10,11... | collective-permute-start | bytes 786440 | tf_op jit(solution)/shard_map/ppermute | solution.py:39
  94.9 25.1 %collective-permute-start.57 = (bf16[256,1152]{1,0:T(8,128)(2,1)S(1)}, bf16[256,1152]{1,0:T(8,128)(2,1)S(1)}, u32[]{:S(2)}, u32[]{:S(2)}) collective-permute-start(bf16[256,1152]{1,0:T(8,128)(2,1)S(1)} %get-tuple-element.195), channel_id=1, source_target_pairs={{0,2},{2,0},{4,6},{6,4},{8,10},{10,8},{12,14},{14,12},{16,18},{18,... | collective-permute-start | bytes 1769480 | tf_op jit(solution)/shard_map/ppermute | solution.py:39
  95.3 26.0 %collective-permute-start.58 = (bf16[256,1152]{1,0:T(8,128)(2,1)S(1)}, bf16[256,1152]{1,0:T(8,128)(2,1)S(1)}, u32[]{:S(2)}, u32[]{:S(2)}) collective-permute-start(bf16[256,1152]{1,0:T(8,128)(2,1)S(1)} %get-tuple-element.196), channel_id=1, source_target_pairs={{0,4},{2,6},{4,0},{6,2},{8,12},{10,14},{12,8},{14,10},{16,20},{18,... | collective-permute-start | bytes 1769480 | tf_op jit(solution)/shard_map/ppermute | solution.py:39
  96.7 28.5 %collective-permute-start.59 = (bf16[256,1152]{1,0:T(8,128)(2,1)S(1)}, bf16[256,1152]{1,0:T(8,128)(2,1)S(1)}, u32[]{:S(2)}, u32[]{:S(2)}) collective-permute-start(bf16[256,1152]{1,0:T(8,128)(2,1)S(1)} %get-tuple-element.197), channel_id=1, source_target_pairs={{0,6},{2,4},{4,2},{6,0},{8,14},{10,12},{12,10},{14,8},{16,22},{18,... | collective-permute-start | bytes 1769480 | tf_op jit(solution)/shard_map/ppermute | solution.py:39
  121.3 50.4 %collective-permute-start.64 = (bf16[256,640]{1,0:T(8,128)(2,1)S(1)}, bf16[256,640]{1,0:T(8,128)(2,1)S(1)}, u32[]{:S(2)}, u32[]{:S(2)}) collective-permute-start(bf16[256,640]{1,0:T(8,128)(2,1)S(1)} %get-tuple-element.205), channel_id=1, source_target_pairs={{0,6},{2,4},{4,2},{6,0},{8,14},{10,12},{12,10},{14,8},{16,22},{18,... | collective-permute-start | bytes 983048 | tf_op jit(solution)/shard_map/ppermute | solution.py:39
  136.6 62.6 %collective-permute-start.60 = (bf16[2,256,1152]{2,1,0:T(8,128)(2,1)S(1)}, bf16[2,256,1152]{2,1,0:T(8,128)(2,1)S(1)}, u32[]{:S(2)}, u32[]{:S(2)}) collective-permute-start(bf16[2,256,1152]{2,1,0:T(8,128)(2,1)S(1)} %get-tuple-element.199), channel_id=1, source_target_pairs={{0,8},{2,10},{4,12},{6,14},{8,0},{10,2},{12,4},{14,6},{16,24},{18,... | collective-permute-start | bytes 3538952 | tf_op jit(solution)/shard_map/ppermute | solution.py:39
  136.7 28.5 %collective-permute-start.26 = (bf16[256,128]{1,0:T(8,128)(2,1)S(1)}, bf16[256,128]{1,0:T(8,128)(2,1)S(1)}, u32[]{:S(2)}, u32[]{:S(2)}) collective-permute-start(bf16[256,128]{1,0:T(8,128)(2,1)S(1)} %get-tuple-element.157), channel_id=1, source_target_pairs={{0,8},{4,12},{8,0},{12,4},{16,24},{20,28},{24,16},{28,20},{1,9},{5... | collective-permute-start | bytes 196616 | tf_op jit(solution)/shard_map/ppermute | solution.py:39
  138.8 27.9 %collective-permute-start.27 = (bf16[256,128]{1,0:T(8,128)(2,1)S(1)}, bf16[256,128]{1,0:T(8,128)(2,1)S(1)}, u32[]{:S(2)}, u32[]{:S(2)}) collective-permute-start(bf16[256,128]{1,0:T(8,128)(2,1)S(1)} %get-tuple-element.158), channel_id=1, source_target_pairs={{0,16},{4,20},{8,24},{12,28},{16,0},{20,4},{24,8},{28,12},{1,17},{... | collective-permute-start | bytes 196616 | tf_op jit(solution)/shard_map/ppermute | solution.py:39
  139.0 29.1 %collective-permute-start.28 = (bf16[256,128]{1,0:T(8,128)(2,1)S(1)}, bf16[256,128]{1,0:T(8,128)(2,1)S(1)}, u32[]{:S(2)}, u32[]{:S(2)}) collective-permute-start(bf16[256,128]{1,0:T(8,128)(2,1)S(1)} %get-tuple-element.159), channel_id=1, source_target_pairs={{0,24},{4,28},{8,16},{12,20},{16,8},{20,12},{24,0},{28,4},{1,25},{... | collective-permute-start | bytes 196616 | tf_op jit(solution)/shard_map/ppermute | solution.py:39
  173.0 16.8 %collective-permute-start.29 = (bf16[256,1024]{1,0:T(8,128)(2,1)S(1)}, bf16[256,1024]{1,0:T(8,128)(2,1)S(1)}, u32[]{:S(2)}, u32[]{:S(2)}) collective-permute-start(bf16[256,1024]{1,0:T(8,128)(2,1)S(1)} %get-tuple-element.164.own_ref), channel_id=1, source_target_pairs={{0,1},{1,0},{2,3},{3,2},{4,5},{5,4},{6,7},{7,6},{8,9},{9,8},{10,11... | collective-permute-start | bytes 1572872 | tf_op jit(solution)/shard_map/ppermute | solution.py:39
  189.8 30.2 %collective-permute-start.65 = (bf16[2,256,640]{2,1,0:T(8,128)(2,1)S(1)}, bf16[2,256,640]{2,1,0:T(8,128)(2,1)S(1)}, u32[]{:S(2)}, u32[]{:S(2)}) collective-permute-start(bf16[2,256,640]{2,1,0:T(8,128)(2,1)S(1)} %get-tuple-element.207), channel_id=1, source_target_pairs={{0,8},{2,10},{4,12},{6,14},{8,0},{10,2},{12,4},{14,6},{16,24},{18,... | collective-permute-start | bytes 1966088 | tf_op jit(solution)/shard_map/ppermute | solution.py:39
  197.2 33.6 %collective-permute-start.46 = (bf16[2,256,512]{2,1,0:T(8,128)(2,1)S(1)}, bf16[2,256,512]{2,1,0:T(8,128)(2,1)S(1)}, u32[]{:S(2)}, u32[]{:S(2)}) collective-permute-start(bf16[2,256,512]{2,1,0:T(8,128)(2,1)S(1)} %get-tuple-element.181), channel_id=1, source_target_pairs={{0,8},{2,10},{4,12},{6,14},{8,0},{10,2},{12,4},{14,6},{16,24},{18,... | collective-permute-start | bytes 1572872 | tf_op jit(solution)/shard_map/ppermute | solution.py:39
  199.9 50.0 %collective-permute-start.61 = (bf16[256,1152]{1,0:T(8,128)(2,1)S(1)}, bf16[256,1152]{1,0:T(8,128)(2,1)S(1)}, u32[]{:S(2)}, u32[]{:S(2)}) collective-permute-start(bf16[256,1152]{1,0:T(8,128)(2,1)S(1)} %get-tuple-element.201), channel_id=1, source_target_pairs={{0,16},{2,18},{4,20},{6,22},{8,24},{10,26},{12,28},{14,30},{16,0},... | collective-permute-start | bytes 1769480 | tf_op jit(solution)/shard_map/ppermute | solution.py:39
  220.7 29.3 %collective-permute-start.66 = (bf16[256,640]{1,0:T(8,128)(2,1)S(1)}, bf16[256,640]{1,0:T(8,128)(2,1)S(1)}, u32[]{:S(2)}, u32[]{:S(2)}) collective-permute-start(bf16[256,640]{1,0:T(8,128)(2,1)S(1)} %get-tuple-element.209), channel_id=1, source_target_pairs={{0,16},{2,18},{4,20},{6,22},{8,24},{10,26},{12,28},{14,30},{16,0},... | collective-permute-start | bytes 983048 | tf_op jit(solution)/shard_map/ppermute | solution.py:39
  231.5 24.0 %collective-permute-start.47 = (bf16[256,512]{1,0:T(8,128)(2,1)S(1)}, bf16[256,512]{1,0:T(8,128)(2,1)S(1)}, u32[]{:S(2)}, u32[]{:S(2)}) collective-permute-start(bf16[256,512]{1,0:T(8,128)(2,1)S(1)} %get-tuple-element.183), channel_id=1, source_target_pairs={{0,16},{2,18},{4,20},{6,22},{8,24},{10,26},{12,28},{14,30},{16,0},... | collective-permute-start | bytes 786440 | tf_op jit(solution)/shard_map/ppermute | solution.py:39
  250.6 19.7 %collective-permute-start.67 = (bf16[64,1792]{1,0:T(8,128)(2,1)S(1)}, bf16[64,1792]{1,0:T(8,128)(2,1)S(1)}, u32[]{:S(2)}, u32[]{:S(2)}) collective-permute-start(bf16[64,1792]{1,0:T(8,128)(2,1)S(1)} %get-tuple-element.211), channel_id=1, source_target_pairs={{0,2},{2,0},{4,6},{6,4},{8,10},{10,8},{12,14},{14,12},{16,18},{18,... | collective-permute-start | bytes 688136 | tf_op jit(solution)/shard_map/ppermute | solution.py:39
  252.3 18.1 %collective-permute-start.68 = (bf16[64,1792]{1,0:T(8,128)(2,1)S(1)}, bf16[64,1792]{1,0:T(8,128)(2,1)S(1)}, u32[]{:S(2)}, u32[]{:S(2)}) collective-permute-start(bf16[64,1792]{1,0:T(8,128)(2,1)S(1)} %get-tuple-element.212), channel_id=1, source_target_pairs={{0,4},{2,6},{4,0},{6,2},{8,12},{10,14},{12,8},{14,10},{16,20},{18,... | collective-permute-start | bytes 688136 | tf_op jit(solution)/shard_map/ppermute | solution.py:39
  252.8 17.6 %collective-permute-start.69 = (bf16[64,1792]{1,0:T(8,128)(2,1)S(1)}, bf16[64,1792]{1,0:T(8,128)(2,1)S(1)}, u32[]{:S(2)}, u32[]{:S(2)}) collective-permute-start(bf16[64,1792]{1,0:T(8,128)(2,1)S(1)} %get-tuple-element.213), channel_id=1, source_target_pairs={{0,6},{2,4},{4,2},{6,0},{8,14},{10,12},{12,10},{14,8},{16,22},{18,... | collective-permute-start | bytes 688136 | tf_op jit(solution)/shard_map/ppermute | solution.py:39
  (68 other events, 701.7 us)

commit v2 on v1

--- a/solution.py
+++ b/solution.py
@@ -41,6 +41,10 @@
 
 def named_swap(value, axis="tp"):
     return xor_swap(value, axis, 1)
+
+
+def stay(value):
+    return pltpu.with_memory_space_constraint(value, pltpu.HBM)
 
 
 def level_swap(parts):
@@ -1062,15 +1066,15 @@
         + [full_block] * kv_heads
         + [head_block] * kv_heads,
         [
-            token_rows,
-            cot_rows,
-            attn_gain_row,
-            w_query,
-            w_key,
-            w_value,
-            q_gain_row,
-            k_gain_row,
-            positions,
+            stay(token_rows),
+            stay(cot_rows),
+            stay(attn_gain_row),
+            stay(w_query),
+            stay(w_key),
+            stay(w_value),
+            stay(q_gain_row),
+            stay(k_gain_row),
+            stay(positions),
         ],
         scalars=(info,),
         scratch=[
@@ -1128,14 +1132,16 @@
         named_swap(attn_part),
         ffn_gain_row,
         cot_rows,
-        w_gate,
-        w_up,
-        w_down,
+        stay(w_gate),
+        stay(w_up),
+        stay(w_down),
     )
     ffn_other = named_swap(ffn_part)
     back_other = named_swap(back_part)
     hidden_plane = plane_swap(hidden_parts)
-    both_plane = plane_swap(both_parts)
+    both_near = [xor_swap(both_parts[1], everywhere, 1)]
+    both_near += [xor_swap(both_parts[flip], everywhere, flip) for flip in (2, 3)]
+    both_plane = [both_parts[0], *both_near]
     two_near, two_far = plane_gather(two_half)
     two_pieces = (normed_two, two_near, two_far, 0)
     half, width = window(hidden_width)

time: 273 us -> 266 us (0.974)
  local copies, waits for them, and re-layouts: 12.9 us -> 0.2 us
  waiting for transfers between devices: 128 us -> 131 us
  Pallas kernels: 57.1 us -> 59.9 us
    unnamed x44 -> x20, local copies, waits for them, and re-layouts: 12.8 us -> 0.04 us
    ppermute x70, waiting for transfers between devices: 128 us -> 131 us  [xor_swap(): lax.ppermute(value, axis, [(index, index ^ flip) for index in range(size)])]
  transfers between devices with their start and end apart: 70 -> 70, of which waited for: 27 -> 27; matrix products, arithmetic and copies ran while one was open for 0% -> 0% of each run, Pallas kernels for 18% -> 19%
where the time goes in v2:
time: 266 us
  waiting for transfers between devices  131 us (49%)
  starting transfers between devices  73 us (27%)
  Pallas kernels  59.9 us (23%)
    ppermute x70, waiting for transfers between devices, xor_swap(): lax.ppermute(value, axis, [(index, index ^ flip) for index in range(size)])  131 us
    ppermute x70, starting transfers between devices, xor_swap(): lax.ppermute(value, axis, [(index, index ^ flip) for index in range(size)])  73 us
    pallas_call x15, Pallas kernels, whole_call(): pl.pallas_call(kernel, out_shape=tuple(outs), in_specs=[smem_spec()] * le...  30.5 us
    pallas_call x3, Pallas kernels, rows(): pl.pallas_call(functools.partial(rows_kernel, shape_jobs, steps), grid_sp...  15.3 us
    pallas_call x1, Pallas kernels, ffn_call(): pl.pallas_call(functools.partial(ffn_kernel, steps), grid_spec=pltpu.Pref...  14.1 us
  transfers between devices with their start and end apart: 70, of which 27 were waited for; matrix products, arithmetic and copies ran while one was open for 0% of the time, Pallas kernels for 19%

profile of v2, /device:TPU:0, one launch (start us, length us, event | category | flops | bytes accessed | tf_op | source)
XLA Modules:
  0.0 265.7 jit_solution(10797938378753545632)
XLA Ops:
  0.8 3.9 %shard_map.237 = (bf16[256,1024]{1,0:T(8,128)(2,1)S(1)}, bf16[128,2048]{1,0:T(8,128)(2,1)S(1)}, f32[256,512]{1,0:T(8,128)S(1)}, f32[256,256]{1,0:T(8,128)S(1)}, ...) custom-call(s32[6]{0:T(128)S(1)} %stack.27.info_ref.refs_0_, ...), custom_call_target="tpu_custom_call" | custom-call | flops 536870912 | bytes 5789184 | tf_op jit(solution)/shard_map/pallas_call | solution.py:246
  4.7 3.1 %collective-permute-start.3 = (bf16[256,128]{1,0:T(8,128)(2,1)S(1)}, bf16[256,128]{1,0:T(8,128)(2,1)S(1)}, u32[]{:S(2)}, u32[]{:S(2)}) collective-permute-start(bf16[256,128]{1,0:T(8,128)(2,1)S(1)} %get-tuple-element.122), channel_id=1, source_target_pairs={{0,8},{4,12},{8,0},{12,4},{16,24},{20,28},{24,16},{28,20},{1,9},{5... | collective-permute-start | bytes 196616 | tf_op jit(solution)/shard_map/ppermute | solution.py:39
  7.8 2.6 collective-permute-start.4
  24.9 4.8 %shard_map.238 = (bf16[4,256,128]{2,1,0:T(8,128)(2,1)S(1)}, f32[8,256]{1,0:T(8,128)S(1)}, bf16[256,128]{1,0:T(8,128)(2,1)S(1)}, bf16[256,128]{1,0:T(8,128)(2,1)S...) custom-call(s32[6]{0:T(128)S(1)} %stack.27.info_ref.refs_0_, ...), custom_call_target="tpu_custom_call" | custom-call | flops 1073741824 | bytes 1335296 | tf_op jit(solution)/shard_map/pallas_call | solution.py:246
  43.7 14.1 %ffn.1 = (f32[256,1024]{1,0:T(8,128)S(1)}, bf16[256,1024]{1,0:T(8,128)(2,1)S(1)}, bf16[128,1024]{1,0:T(8,128)(2,1)S(1)}, bf16[256,1024]{1,0:T(8,128)(2,1)S(1)}, ...) custom-call(s32[6]{0:T(128)S(1)} %stack.27.info_ref.refs_0_, ...), custom_call_target="tpu_custom_call" | custom-call | flops 9663676416 | bytes 14155776 | tf_op jit(solution)/shard_map/ffn/pallas_call | solution.py:589
  61.4 6.0 %collective-permute-done.38.refs_17_.refs_3_ = bf16[128,2048]{1,0:T(8,128)(2,1)S(1)} collective-permute-done((bf16[128,2048]{1,0:T(8,128)(2,1)S(1)}, bf16[128,2048]{1,0:T(8,128)(2,1)S(1)}, u32[]{:S(2)}, u32[]{:S(2)}) %collective-permute-start.38) | collective-permute-done | bytes 524320 | tf_op jit(solution)/shard_map/ppermute | solution.py:39
  67.3 5.5 %collective-permute-done.51.refs_1_ = bf16[128,1024]{1,0:T(8,128)(2,1)S(1)} collective-permute-done((bf16[128,1024]{1,0:T(8,128)(2,1)S(1)}, bf16[128,1024]{1,0:T(8,128)(2,1)S(1)}, u32[]{:S(2)}, u32[]{:S(2)}) %collective-permute-start.51) | collective-permute-done | bytes 262176 | tf_op jit(solution)/shard_map/ppermute | solution.py:39
  73.4 4.7 %collective-permute-done.53.refs_3_ = bf16[128,1024]{1,0:T(8,128)(2,1)S(1)} collective-permute-done((bf16[128,1024]{1,0:T(8,128)(2,1)S(1)}, bf16[128,1024]{1,0:T(8,128)(2,1)S(1)}, u32[]{:S(2)}, u32[]{:S(2)}) %collective-permute-start.53) | collective-permute-done | bytes 262176 | tf_op jit(solution)/shard_map/ppermute | solution.py:39
  79.9 8.3 %collective-permute-done.62.refs_8_ = bf16[256,640]{1,0:T(8,128)(2,1)S(1)} collective-permute-done((bf16[256,640]{1,0:T(8,128)(2,1)S(1)}, bf16[256,640]{1,0:T(8,128)(2,1)S(1)}, u32[]{:S(2)}, u32[]{:S(2)}) %collective-permute-start.62) | collective-permute-done | bytes 327712 | tf_op jit(solution)/shard_map/ppermute | solution.py:39
  91.7 2.8 %shard_map.240 = (f32[256,1024]{1,0:T(8,128)}, f32[256,1024]{1,0:T(8,128)S(1)}, bf16[256,1024]{1,0:T(8,128)(2,1)S(1)}, f32[8,1024]{1,0:T(8,128)S(1)}, bf16[128,1...) custom-call(s32[6]{0:T(128)S(1)} %stack.27.info_ref.refs_0_, ...), custom_call_target="tpu_custom_call" | custom-call | flops 268435456 | bytes 8818688 | tf_op jit(solution)/shard_map/pallas_call | solution.py:246
  104.8 6.4 %shard_map.241 = (bf16[256,128]{1,0:T(8,128)(2,1)S(1)}, bf16[256,128]{1,0:T(8,128)(2,1)S(1)}, bf16[256,128]{1,0:T(8,128)(2,1)S(1)}, bf16[256,128]{1,0:T(8,128)(2...) custom-call(s32[6]{0:T(128)S(1)} %stack.27.info_ref.refs_0_, ...), custom_call_target="tpu_custom_call" | custom-call | flops 2684354560 | bytes 2383872 | tf_op jit(solution)/shard_map/pallas_call | solution.py:246
  115.2 3.2 %collective-permute-done.59.refs_10_ = bf16[256,1152]{1,0:T(8,128)(2,1)S(1)} collective-permute-done((bf16[256,1152]{1,0:T(8,128)(2,1)S(1)}, bf16[256,1152]{1,0:T(8,128)(2,1)S(1)}, u32[]{:S(2)}, u32[]{:S(2)}) %collective-permute-start.59) | collective-permute-done | bytes 589856 | tf_op jit(solution)/shard_map/ppermute | solution.py:39
  124.2 5.6 %rows.4 = (bf16[2,256,1152]{2,1,0:T(8,128)(2,1)S(1)}, f32[2,256,1152]{2,1,0:T(8,128)S(1)}) custom-call(s32[6]{0:T(128)S(1)} %stack.27.info_ref.refs_0_, bf16[256,1024]{1,0:T(8,128)(2,1)S(1)} %get-tuple-element.192.refs_0_, bf16[128,1024]{1,0:T(8,128)(2,1)S(1)} %collective-permute-done.51.refs_1_, bf16[128,1024]{1,0:T(8,128)(2,1)S(1)} %collective-permute-done.52.refs_2_, ...), custom_call_target="tpu_custom_call" | custom-call | flops 2415919104 | bytes 8007680 | tf_op jit(solution)/shard_map/rows/pallas_call | solution.py:913
  134.5 24.0 %collective-permute-done.26.refs_5_ = bf16[256,128]{1,0:T(8,128)(2,1)S(1)} collective-permute-done((bf16[256,128]{1,0:T(8,128)(2,1)S(1)}, bf16[256,128]{1,0:T(8,128)(2,1)S(1)}, u32[]{:S(2)}, u32[]{:S(2)}) %collective-permute-start.26) | collective-permute-done | bytes 65568 | tf_op jit(solution)/shard_map/ppermute | solution.py:39
  162.0 3.0 %shard_map.243 = (bf16[256,1024]{1,0:T(8,128)(2,1)S(1)}, f32[8,128]{1,0:T(8,128)S(1)}, bf16[256,256]{1,0:T(8,128)(2,1)S(1)}, bf16[256,256]{1,0:T(8,128)(2,1)S(1)...) custom-call(s32[6]{0:T(128)S(1)} %stack.27.info_ref.refs_0_, ...), custom_call_target="tpu_custom_call" | custom-call | flops 536870912 | bytes 4723200 | tf_op jit(solution)/shard_map/pallas_call | solution.py:246
  166.4 2.6 collective-permute-done.30.refs_1_.refs_8_.refs_9_
  171.9 3.5 %collective-permute-done.32.refs_3_.refs_12_.refs_13_ = bf16[128,1280]{1,0:T(8,128)(2,1)S(1)} collective-permute-done((bf16[128,1280]{1,0:T(8,128)(2,1)S(1)}, bf16[128,1280]{1,0:T(8,128)(2,1)S(1)}, u32[]{:S(2)}, u32[]{:S(2)}) %collective-permute-start.32) | collective-permute-done | bytes 327712 | tf_op jit(solution)/shard_map/ppermute | solution.py:39
  175.4 2.8 %collective-permute-start.44 = (bf16[256,256]{1,0:T(8,128)(2,1)S(1)}, bf16[256,256]{1,0:T(8,128)(2,1)S(1)}, u32[]{:S(2)}, u32[]{:S(2)}) collective-permute-start(bf16[256,256]{1,0:T(8,128)(2,1)S(1)} %get-tuple-element.176), channel_id=1, source_target_pairs={{0,6},{2,4},{4,2},{6,0},{8,14},{10,12},{12,10},{14,8},{16,22},{18,... | collective-permute-start | bytes 393224 | tf_op jit(solution)/shard_map/ppermute | solution.py:39
  178.2 4.1 %rows.5 = (bf16[2,256,640]{2,1,0:T(8,128)(2,1)S(1)}, f32[2,256,640]{2,1,0:T(8,128)S(1)}) custom-call(s32[6]{0:T(128)S(1)} %stack.27.info_ref.refs_0_, bf16[256,1024]{1,0:T(8,128)(2,1)S(1)} %bitcast.21, bf16[128,2048]{1,0:T(8,128)(2,1)S(1)} %collective-permute-done.36.refs_15_.refs_1_, bf16[128,2048]{1,0:T(8,128)(2,1)S(1)} %collective-permute-done.37.refs_16_.refs_2_, ...), custom_call_target="tpu_custom_call" | custom-call | flops 1342177280 | bytes 6959104 | tf_op jit(solution)/shard_map/rows/pallas_call | solution.py:913
  185.0 5.6 %rows.3 = (bf16[2,256,512]{2,1,0:T(8,128)(2,1)S(1)}, f32[2,256,512]{2,1,0:T(8,128)S(1)}) custom-call(s32[6]{0:T(128)S(1)} %stack.27.info_ref.refs_0_, bf16[256,1024]{1,0:T(8,128)(2,1)S(1)} %get-tuple-element.166.refs_0_, bf16[128,1280]{1,0:T(8,128)(2,1)S(1)} %collective-permute-done.30.refs_1_.refs_8_.refs_9_, ...), custom_call_target="tpu_custom_call" | custom-call | flops 805306368 | bytes 10358784 | tf_op jit(solution)/shard_map/rows/pallas_call | solution.py:913
  193.3 20.0 %collective-permute-done.65.found_ref = bf16[2,256,640]{2,1,0:T(8,128)(2,1)S(1)} collective-permute-done((bf16[2,256,640]{2,1,0:T(8,128)(2,1)S(1)}, bf16[2,256,640]{2,1,0:T(8,128)(2,1)S(1)}, u32[]{:S(2)}, u32[]{:S(2)}) %collective-permute-start.65) | collective-permute-done | bytes 655392 | tf_op jit(solution)/shard_map/ppermute | solution.py:39
  214.1 10.0 %collective-permute-done.46.found_ref = bf16[2,256,512]{2,1,0:T(8,128)(2,1)S(1)} collective-permute-done((bf16[2,256,512]{2,1,0:T(8,128)(2,1)S(1)}, bf16[2,256,512]{2,1,0:T(8,128)(2,1)S(1)}, u32[]{:S(2)}, u32[]{:S(2)}) %collective-permute-start.46) | collective-permute-done | bytes 524320 | tf_op jit(solution)/shard_map/ppermute | solution.py:39
  224.8 18.4 %collective-permute-done.66.refs_3_ = bf16[256,640]{1,0:T(8,128)(2,1)S(1)} collective-permute-done((bf16[256,640]{1,0:T(8,128)(2,1)S(1)}, bf16[256,640]{1,0:T(8,128)(2,1)S(1)}, u32[]{:S(2)}, u32[]{:S(2)}) %collective-permute-start.66) | collective-permute-done | bytes 327712 | tf_op jit(solution)/shard_map/ppermute | solution.py:39
  251.5 5.6 %collective-permute-done.48.refs_1_ = bf16[64,512]{1,0:T(8,128)(2,1)S(1)} collective-permute-done((bf16[64,512]{1,0:T(8,128)(2,1)S(1)}, bf16[64,512]{1,0:T(8,128)(2,1)S(1)}, u32[]{:S(2)}, u32[]{:S(2)}) %collective-permute-start.48) | collective-permute-done | bytes 65568 | tf_op jit(solution)/shard_map/ppermute | solution.py:39
  (160 shorter events, 94.0 us)
Async XLA Ops:
  40.2 20.3 %collective-permute-start.37 = (bf16[128,2048]{1,0:T(8,128)(2,1)S(1)}, bf16[128,2048]{1,0:T(8,128)(2,1)S(1)}, u32[]{:S(2)}, u32[]{:S(2)}) collective-permute-start(bf16[128,2048]{1,0:T(8,128)(2,1)S(1)} %get-tuple-element.172), channel_id=1, source_target_pairs={{0,4},{2,6},{4,0},{6,2},{8,12},{10,14},{12,8},{14,10},{16,20},{18,... | collective-permute-start | bytes 1572872 | tf_op jit(solution)/shard_map/ppermute | solution.py:39
  41.6 25.7 %collective-permute-start.38 = (bf16[128,2048]{1,0:T(8,128)(2,1)S(1)}, bf16[128,2048]{1,0:T(8,128)(2,1)S(1)}, u32[]{:S(2)}, u32[]{:S(2)}) collective-permute-start(bf16[128,2048]{1,0:T(8,128)(2,1)S(1)} %get-tuple-element.172), channel_id=1, source_target_pairs={{0,6},{2,4},{4,2},{6,0},{8,14},{10,12},{12,10},{14,8},{16,22},{18,... | collective-permute-start | bytes 1572872 | tf_op jit(solution)/shard_map/ppermute | solution.py:39
  43.6 34.4 %collective-permute-start.39 = (bf16[128,2048]{1,0:T(8,128)(2,1)S(1)}, bf16[128,2048]{1,0:T(8,128)(2,1)S(1)}, u32[]{:S(2)}, u32[]{:S(2)}) collective-permute-start(bf16[128,2048]{1,0:T(8,128)(2,1)S(1)} %collective-permute-done.36.refs_15_.refs_1_), channel_id=1, source_target_pairs={{0,1},{1,0},{2,3},{3,2},{4,5},{5,4},{6,7},{7,6},{8,9},{9,8},{10,11... | collective-permute-start | bytes 1572872 | tf_op jit(solution)/shard_map/ppermute | solution.py:39
  60.5 17.6 %collective-permute-start.53 = (bf16[128,1024]{1,0:T(8,128)(2,1)S(1)}, bf16[128,1024]{1,0:T(8,128)(2,1)S(1)}, u32[]{:S(2)}, u32[]{:S(2)}) collective-permute-start(bf16[128,1024]{1,0:T(8,128)(2,1)S(1)} %get-tuple-element.193), channel_id=1, source_target_pairs={{0,6},{2,4},{4,2},{6,0},{8,14},{10,12},{12,10},{14,8},{16,22},{18,... | collective-permute-start | bytes 786440 | tf_op jit(solution)/shard_map/ppermute | solution.py:39
  72.9 15.8 %collective-permute-start.14 = (bf16[256,1024]{1,0:T(8,128)(2,1)S(1)}, bf16[256,1024]{1,0:T(8,128)(2,1)S(1)}, u32[]{:S(2)}, u32[]{:S(2)}) collective-permute-start(bf16[256,1024]{1,0:T(8,128)(2,1)S(1)} %get-tuple-element.131.ffn_own_ref), channel_id=1, source_target_pairs={{0,1},{1,0},{2,3},{3,2},{4,5},{5,4},{6,7},{7,6},{8,9},{9,8},{10,11... | collective-permute-start | bytes 1572872 | tf_op jit(solution)/shard_map/ppermute | solution.py:39
  78.5 15.9 %collective-permute-start.63 = (bf16[256,640]{1,0:T(8,128)(2,1)S(1)}, bf16[256,640]{1,0:T(8,128)(2,1)S(1)}, u32[]{:S(2)}, u32[]{:S(2)}) collective-permute-start(bf16[256,640]{1,0:T(8,128)(2,1)S(1)} %get-tuple-element.204), channel_id=1, source_target_pairs={{0,4},{2,6},{4,0},{6,2},{8,12},{10,14},{12,8},{14,10},{16,20},{18,... | collective-permute-start | bytes 983048 | tf_op jit(solution)/shard_map/ppermute | solution.py:39
  79.9 15.3 %collective-permute-start.54 = (bf16[128,1024]{1,0:T(8,128)(2,1)S(1)}, bf16[128,1024]{1,0:T(8,128)(2,1)S(1)}, u32[]{:S(2)}, u32[]{:S(2)}) collective-permute-start(bf16[128,1024]{1,0:T(8,128)(2,1)S(1)} %collective-permute-done.51.refs_1_), channel_id=1, source_target_pairs={{0,1},{1,0},{2,3},{3,2},{4,5},{5,4},{6,7},{7,6},{8,9},{9,8},{10,11... | collective-permute-start | bytes 786440 | tf_op jit(solution)/shard_map/ppermute | solution.py:39
  88.2 25.1 %collective-permute-start.57 = (bf16[256,1152]{1,0:T(8,128)(2,1)S(1)}, bf16[256,1152]{1,0:T(8,128)(2,1)S(1)}, u32[]{:S(2)}, u32[]{:S(2)}) collective-permute-start(bf16[256,1152]{1,0:T(8,128)(2,1)S(1)} %get-tuple-element.195), channel_id=1, source_target_pairs={{0,2},{2,0},{4,6},{6,4},{8,10},{10,8},{12,14},{14,12},{16,18},{18,... | collective-permute-start | bytes 1769480 | tf_op jit(solution)/shard_map/ppermute | solution.py:39
  88.7 25.9 %collective-permute-start.58 = (bf16[256,1152]{1,0:T(8,128)(2,1)S(1)}, bf16[256,1152]{1,0:T(8,128)(2,1)S(1)}, u32[]{:S(2)}, u32[]{:S(2)}) collective-permute-start(bf16[256,1152]{1,0:T(8,128)(2,1)S(1)} %get-tuple-element.196), channel_id=1, source_target_pairs={{0,4},{2,6},{4,0},{6,2},{8,12},{10,14},{12,8},{14,10},{16,20},{18,... | collective-permute-start | bytes 1769480 | tf_op jit(solution)/shard_map/ppermute | solution.py:39
  90.0 28.5 %collective-permute-start.59 = (bf16[256,1152]{1,0:T(8,128)(2,1)S(1)}, bf16[256,1152]{1,0:T(8,128)(2,1)S(1)}, u32[]{:S(2)}, u32[]{:S(2)}) collective-permute-start(bf16[256,1152]{1,0:T(8,128)(2,1)S(1)} %get-tuple-element.197), channel_id=1, source_target_pairs={{0,6},{2,4},{4,2},{6,0},{8,14},{10,12},{12,10},{14,8},{16,22},{18,... | collective-permute-start | bytes 1769480 | tf_op jit(solution)/shard_map/ppermute | solution.py:39
  114.6 50.4 %collective-permute-start.64 = (bf16[256,640]{1,0:T(8,128)(2,1)S(1)}, bf16[256,640]{1,0:T(8,128)(2,1)S(1)}, u32[]{:S(2)}, u32[]{:S(2)}) collective-permute-start(bf16[256,640]{1,0:T(8,128)(2,1)S(1)} %get-tuple-element.205), channel_id=1, source_target_pairs={{0,6},{2,4},{4,2},{6,0},{8,14},{10,12},{12,10},{14,8},{16,22},{18,... | collective-permute-start | bytes 983048 | tf_op jit(solution)/shard_map/ppermute | solution.py:39
  129.9 62.6 %collective-permute-start.60 = (bf16[2,256,1152]{2,1,0:T(8,128)(2,1)S(1)}, bf16[2,256,1152]{2,1,0:T(8,128)(2,1)S(1)}, u32[]{:S(2)}, u32[]{:S(2)}) collective-permute-start(bf16[2,256,1152]{2,1,0:T(8,128)(2,1)S(1)} %get-tuple-element.199), channel_id=1, source_target_pairs={{0,8},{2,10},{4,12},{6,14},{8,0},{10,2},{12,4},{14,6},{16,24},{18,... | collective-permute-start | bytes 3538952 | tf_op jit(solution)/shard_map/ppermute | solution.py:39
  130.0 28.5 %collective-permute-start.26 = (bf16[256,128]{1,0:T(8,128)(2,1)S(1)}, bf16[256,128]{1,0:T(8,128)(2,1)S(1)}, u32[]{:S(2)}, u32[]{:S(2)}) collective-permute-start(bf16[256,128]{1,0:T(8,128)(2,1)S(1)} %get-tuple-element.157), channel_id=1, source_target_pairs={{0,8},{4,12},{8,0},{12,4},{16,24},{20,28},{24,16},{28,20},{1,9},{5... | collective-permute-start | bytes 196616 | tf_op jit(solution)/shard_map/ppermute | solution.py:39
  132.1 27.9 %collective-permute-start.27 = (bf16[256,128]{1,0:T(8,128)(2,1)S(1)}, bf16[256,128]{1,0:T(8,128)(2,1)S(1)}, u32[]{:S(2)}, u32[]{:S(2)}) collective-permute-start(bf16[256,128]{1,0:T(8,128)(2,1)S(1)} %get-tuple-element.158), channel_id=1, source_target_pairs={{0,16},{4,20},{8,24},{12,28},{16,0},{20,4},{24,8},{28,12},{1,17},{... | collective-permute-start | bytes 196616 | tf_op jit(solution)/shard_map/ppermute | solution.py:39
  132.3 29.0 %collective-permute-start.28 = (bf16[256,128]{1,0:T(8,128)(2,1)S(1)}, bf16[256,128]{1,0:T(8,128)(2,1)S(1)}, u32[]{:S(2)}, u32[]{:S(2)}) collective-permute-start(bf16[256,128]{1,0:T(8,128)(2,1)S(1)} %get-tuple-element.159), channel_id=1, source_target_pairs={{0,24},{4,28},{8,16},{12,20},{16,8},{20,12},{24,0},{28,4},{1,25},{... | collective-permute-start | bytes 196616 | tf_op jit(solution)/shard_map/ppermute | solution.py:39
  166.3 16.8 %collective-permute-start.29 = (bf16[256,1024]{1,0:T(8,128)(2,1)S(1)}, bf16[256,1024]{1,0:T(8,128)(2,1)S(1)}, u32[]{:S(2)}, u32[]{:S(2)}) collective-permute-start(bf16[256,1024]{1,0:T(8,128)(2,1)S(1)} %get-tuple-element.164.own_ref), channel_id=1, source_target_pairs={{0,1},{1,0},{2,3},{3,2},{4,5},{5,4},{6,7},{7,6},{8,9},{9,8},{10,11... | collective-permute-start | bytes 1572872 | tf_op jit(solution)/shard_map/ppermute | solution.py:39
  183.1 30.2 %collective-permute-start.65 = (bf16[2,256,640]{2,1,0:T(8,128)(2,1)S(1)}, bf16[2,256,640]{2,1,0:T(8,128)(2,1)S(1)}, u32[]{:S(2)}, u32[]{:S(2)}) collective-permute-start(bf16[2,256,640]{2,1,0:T(8,128)(2,1)S(1)} %get-tuple-element.207), channel_id=1, source_target_pairs={{0,8},{2,10},{4,12},{6,14},{8,0},{10,2},{12,4},{14,6},{16,24},{18,... | collective-permute-start | bytes 1966088 | tf_op jit(solution)/shard_map/ppermute | solution.py:39
  190.5 33.6 %collective-permute-start.46 = (bf16[2,256,512]{2,1,0:T(8,128)(2,1)S(1)}, bf16[2,256,512]{2,1,0:T(8,128)(2,1)S(1)}, u32[]{:S(2)}, u32[]{:S(2)}) collective-permute-start(bf16[2,256,512]{2,1,0:T(8,128)(2,1)S(1)} %get-tuple-element.181), channel_id=1, source_target_pairs={{0,8},{2,10},{4,12},{6,14},{8,0},{10,2},{12,4},{14,6},{16,24},{18,... | collective-permute-start | bytes 1572872 | tf_op jit(solution)/shard_map/ppermute | solution.py:39
  193.2 50.1 %collective-permute-start.61 = (bf16[256,1152]{1,0:T(8,128)(2,1)S(1)}, bf16[256,1152]{1,0:T(8,128)(2,1)S(1)}, u32[]{:S(2)}, u32[]{:S(2)}) collective-permute-start(bf16[256,1152]{1,0:T(8,128)(2,1)S(1)} %get-tuple-element.201), channel_id=1, source_target_pairs={{0,16},{2,18},{4,20},{6,22},{8,24},{10,26},{12,28},{14,30},{16,0},... | collective-permute-start | bytes 1769480 | tf_op jit(solution)/shard_map/ppermute | solution.py:39
  214.0 29.3 %collective-permute-start.66 = (bf16[256,640]{1,0:T(8,128)(2,1)S(1)}, bf16[256,640]{1,0:T(8,128)(2,1)S(1)}, u32[]{:S(2)}, u32[]{:S(2)}) collective-permute-start(bf16[256,640]{1,0:T(8,128)(2,1)S(1)} %get-tuple-element.209), channel_id=1, source_target_pairs={{0,16},{2,18},{4,20},{6,22},{8,24},{10,26},{12,28},{14,30},{16,0},... | collective-permute-start | bytes 983048 | tf_op jit(solution)/shard_map/ppermute | solution.py:39
  224.8 24.1 %collective-permute-start.47 = (bf16[256,512]{1,0:T(8,128)(2,1)S(1)}, bf16[256,512]{1,0:T(8,128)(2,1)S(1)}, u32[]{:S(2)}, u32[]{:S(2)}) collective-permute-start(bf16[256,512]{1,0:T(8,128)(2,1)S(1)} %get-tuple-element.183), channel_id=1, source_target_pairs={{0,16},{2,18},{4,20},{6,22},{8,24},{10,26},{12,28},{14,30},{16,0},... | collective-permute-start | bytes 786440 | tf_op jit(solution)/shard_map/ppermute | solution.py:39
  244.0 19.7 %collective-permute-start.67 = (bf16[64,1792]{1,0:T(8,128)(2,1)S(1)}, bf16[64,1792]{1,0:T(8,128)(2,1)S(1)}, u32[]{:S(2)}, u32[]{:S(2)}) collective-permute-start(bf16[64,1792]{1,0:T(8,128)(2,1)S(1)} %get-tuple-element.211), channel_id=1, source_target_pairs={{0,2},{2,0},{4,6},{6,4},{8,10},{10,8},{12,14},{14,12},{16,18},{18,... | collective-permute-start | bytes 688136 | tf_op jit(solution)/shard_map/ppermute | solution.py:39
  245.6 18.1 %collective-permute-start.68 = (bf16[64,1792]{1,0:T(8,128)(2,1)S(1)}, bf16[64,1792]{1,0:T(8,128)(2,1)S(1)}, u32[]{:S(2)}, u32[]{:S(2)}) collective-permute-start(bf16[64,1792]{1,0:T(8,128)(2,1)S(1)} %get-tuple-element.212), channel_id=1, source_target_pairs={{0,4},{2,6},{4,0},{6,2},{8,12},{10,14},{12,8},{14,10},{16,20},{18,... | collective-permute-start | bytes 688136 | tf_op jit(solution)/shard_map/ppermute | solution.py:39
  246.1 17.7 %collective-permute-start.69 = (bf16[64,1792]{1,0:T(8,128)(2,1)S(1)}, bf16[64,1792]{1,0:T(8,128)(2,1)S(1)}, u32[]{:S(2)}, u32[]{:S(2)}) collective-permute-start(bf16[64,1792]{1,0:T(8,128)(2,1)S(1)} %get-tuple-element.213), channel_id=1, source_target_pairs={{0,6},{2,4},{4,2},{6,0},{8,14},{10,12},{12,10},{14,8},{16,22},{18,... | collective-permute-start | bytes 688136 | tf_op jit(solution)/shard_map/ppermute | solution.py:39
  (56 other events, 654.1 us)
